TPU v7x, 32 devices: a whole 2x2x4 slice. The times are simulated.
32 devices in a mesh: replica: 2 (over x), shard: 16 (over z, y, core).
Axes of the slice: x: 2, y: 2, z: 4, core: 2. Of those that a mesh axis runs over, the one named last changes fastest.
Arguments:
- tokens: bfloat16 [6144, 2048], P(('replica', 'shard')), may hold values from -6 to 6
- seg_ids: int32 [6144], P(('replica', 'shard')), may hold values from 0 to 23, as said below
- cotangent: bfloat16 [6144, 2048], P(('replica', 'shard')), may hold values from -6 to 6
- w_in: float32 [2048, 14336], P('shard')
- w_out: float32 [2048, 2048], P('shard'), may hold values from -0.75 to 0.75
- w_fc2: float32 [8192, 2048], P('shard'), may hold values from -0.0625 to 0.0625
- vectors: float32 [22528], P('shard')
- m_in: float32 [2048, 14336], P('shard'), may hold values from -6 to 6
- v_in: float32 [2048, 14336], P('shard'), may hold values from 0.6144 to 6.144
- m_out: float32 [2048, 2048], P('shard'), may hold values from -6 to 6
- v_out: float32 [2048, 2048], P('shard'), may hold values from 0.6144 to 6.144
- m_fc2: float32 [8192, 2048], P('shard'), may hold values from -6 to 6
- v_fc2: float32 [8192, 2048], P('shard'), may hold values from 0.6144 to 6.144
- m_vec: float32 [22528], P('shard'), may hold values from -6 to 6
- v_vec: float32 [22528], P('shard'), may hold values from 0.6144 to 6.144
Outputs:
- output: bfloat16 [6144, 2048], P(('replica', 'shard'))
- grad_tokens: float32 [6144, 2048], P(('replica', 'shard'))
- grad_in: float32 [2048, 14336], P('shard')
- grad_out: float32 [2048, 2048], P('shard')
- grad_fc2: float32 [8192, 2048], P('shard')
- grad_vec: float32 [22528], P('shard')
- new_in: float32 [2048, 14336], P('shard')
- new_out: float32 [2048, 2048], P('shard')
- new_fc2: float32 [8192, 2048], P('shard')
- new_vec: float32 [22528], P('shard')
- new_m_in: float32 [2048, 14336], P('shard')
- new_v_in: float32 [2048, 14336], P('shard')
- new_m_out: float32 [2048, 2048], P('shard')
- new_v_out: float32 [2048, 2048], P('shard')
- new_m_fc2: float32 [8192, 2048], P('shard')
- new_v_fc2: float32 [8192, 2048], P('shard')
- new_m_vec: float32 [22528], P('shard')
- new_v_vec: float32 [22528], P('shard')
Inputs may be any that keep to these rules, and one draw needn't show every extreme that they name: `seg_ids`: within each device's block of 192 consecutive tokens the ids start at 0 and never fall; a run of equal ids is one sequence, so no sequence crosses a block. Some block holds a single sequence of 192 tokens, and some block holds sequences of 8 tokens each.
All inputs are finite; a program needn't handle non-finite values.
Results may differ from a plain program's by a relative error of at most 0.004.
The roundings to bfloat16 on the way count: a program that leaves them out, or rounds other values in their place, can miss the bound.
Values may be sent and summed in bfloat16 or wider, within the bound.
No kernel may reach another device: no remote copies, remote signals or barrier semaphores. Data moves between devices by JAX's collectives and lax.ppermute only.
A program may use at most 640 MiB of HBM per device.

v0:
```python
import jax
import jax.numpy as jnp
from jax import lax
from jax.experimental import pallas as pl
from jax.experimental.pallas import tpu as pltpu
from jax.sharding import PartitionSpec as P


D = 2048
FF = 8192
HEAD = 64
ROT = 32
ADAM_STEP = 4

NORM_EPS = 1e-05
SCORE_SCALE = 0.125
LEARN_RATE = 0.02
BETA_ONE = 0.9
BETA_TWO = 0.98
ADAM_EPS = 1e-08
DECAY = 0.1

RANKS = 16
NZ = 4
CHUNKS = (0, 3, 2, 1)
GRAD_ORDER = (2, 3, 1, 0)
EARLY = 2
QCOL = D // RANKS
FCOL = FF // RANKS
PROJ = 3 * QCOL + FCOL
PAIR = QCOL + FCOL
LOW = jnp.bfloat16
F32 = jnp.float32
BY_LAST = (((1,), (1,)), ((), ()))
BY_FIRST = (((0,), (0,)), ((), ()))


def adamw(weight, grad, first, second, decay):
    first = BETA_ONE * first + (1.0 - BETA_ONE) * grad
    second = BETA_TWO * second + (1.0 - BETA_TWO) * grad * grad
    first_hat = first / (1.0 - BETA_ONE**ADAM_STEP)
    second_hat = second / (1.0 - BETA_TWO**ADAM_STEP)
    weight = weight - LEARN_RATE * (first_hat / (jnp.sqrt(second_hat) + ADAM_EPS) + decay * weight)
    return (weight, first, second)


def dot(a, b, dims=(((1,), (0,)), ((), ()))):
    return lax.dot_general(a, b, dims, preferred_element_type=F32)


def turn(x, cosine, sin_low, sin_high):
    half = ROT // 2
    return x * cosine - pltpu.roll(x, QCOL - half, 1) * sin_low + pltpu.roll(x, half, 1) * sin_high


def block_middle(proj, gh, bias, cosine, sine, segc, segr, ah_ref, gp_ref, sum_ref, rows):
    length = proj.shape[0]
    half = ROT // 2
    lane = lax.broadcasted_iota(jnp.int32, (length, QCOL), 1)
    inner = lane % HEAD
    sin_low = jnp.where(inner < half, sine, 0.0)
    sin_high = jnp.where(inner >= half, sine, 0.0)
    q = turn(proj[:, :QCOL] + bias[:, :QCOL], cosine, sin_low, sin_high).astype(LOW)
    k = turn(
        proj[:, QCOL : 2 * QCOL] + bias[:, QCOL : 2 * QCOL], cosine, sin_low, sin_high
    ).astype(LOW)
    v = (proj[:, 2 * QCOL : 3 * QCOL] + bias[:, 2 * QCOL : 3 * QCOL]).astype(LOW)
    ga = gh[:, :QCOL].astype(LOW)
    row = lax.broadcasted_iota(jnp.int32, (length, length), 0)
    col = lax.broadcasted_iota(jnp.int32, (length, length), 1)
    allowed = (segc == segr) & (col <= row)
    zero = jnp.zeros((length, QCOL), LOW)
    attended = jnp.zeros((length, QCOL), F32)
    dq = jnp.zeros((length, QCOL), F32)
    dk = jnp.zeros((length, QCOL), F32)
    dv = jnp.zeros((length, QCOL), F32)
    for head in range(QCOL // HEAD):
        mine = (lane >= head * HEAD) & (lane < (head + 1) * HEAD)
        qh = jnp.where(mine, q, zero)
        kh = jnp.where(mine, k, zero)
        vh = jnp.where(mine, v, zero)
        gah = jnp.where(mine, ga, zero)
        scores = jnp.where(allowed, dot(qh, k, BY_LAST) * SCORE_SCALE, -1e30)
        peak = jnp.max(scores, axis=1, keepdims=True)
        grown = jnp.exp(scores - peak)
        probs = grown / jnp.sum(grown, axis=1, keepdims=True)
        low = probs.astype(LOW)
        attended = attended + dot(low, vh)
        dp = dot(gah, v, BY_LAST)
        dv = dv + dot(low, gah, BY_FIRST)
        ds = (probs * (dp - jnp.sum(probs * dp, axis=1, keepdims=True))).astype(LOW)
        dq = dq + dot(ds, kh)
        dk = dk + dot(ds, qh, BY_FIRST)
    ah_ref[rows, :QCOL] = attended.astype(LOW)
    dq = turn(dq * SCORE_SCALE, cosine, -sin_low, -sin_high).astype(LOW)
    dk = turn(dk * SCORE_SCALE, cosine, -sin_low, -sin_high).astype(LOW)
    dv = dv.astype(LOW)
    u = proj[:, 3 * QCOL :] + bias[:, 3 * QCOL :]
    c0 = 0.7978845608028654
    c1 = 0.044715
    square = u * u
    bent = jnp.tanh(c0 * (u + c1 * square * u))
    lift = 0.5 * (1.0 + bent)
    ah_ref[rows, QCOL:] = (u * lift).astype(LOW)
    slope = lift + 0.5 * u * (1.0 - bent * bent) * (c0 * (1.0 + 3.0 * c1 * square))
    df = (gh[:, QCOL:] * slope).astype(LOW)
    for at, part in ((0, dq), (QCOL, dk), (2 * QCOL, dv), (3 * QCOL, df)):
        width = part.shape[1]
        gp_ref[rows, at : at + width] = part
        sum_ref[:, at : at + width] += jnp.sum(part.astype(F32), axis=0, keepdims=True)


def chunk_kernel(
    n_own, n_y, n_c, n_cy, g_own, g_y, g_c, g_cy, w_cols, w_pair, bias, tail, cosine, sine, segc, segr,
    n_cat, g_cat, ah_out, gp_out, far_out, near_out, sums,
    n_s, g_s, gh_s, proj_s, ah_s, gp_s, far_s, near_s, in_sem, out_sem,
):
    length = n_own.shape[0]
    rows = 4 * length
    near = rows // 2
    wide = 256

    def into(pieces, held, sem):
        copies = [
            pltpu.make_async_copy(ref, held.at[pl.ds(i * length, length)], sem.at[i])
            for i, ref in enumerate(pieces)
        ]
        for one in copies:
            one.start()
        return copies

    g_in = into((g_own, g_y, g_c, g_cy), g_s, in_sem.at[0])
    n_in = into((n_own, n_y, n_c, n_cy), n_s, in_sem.at[1])
    for one in g_in:
        one.wait()
    drains = [pltpu.make_async_copy(g_s, g_cat, out_sem.at[0])]
    drains[-1].start()
    for at in range(0, PAIR, wide):
        upto = min(at + wide, PAIR)
        gh_s[:, at:upto] = dot(g_s[...], w_pair[at:upto, :], BY_LAST)
    for one in n_in:
        one.wait()
    drains.append(pltpu.make_async_copy(n_s, n_cat, out_sem.at[1]))
    drains[-1].start()
    for at in range(0, PROJ, wide):
        upto = min(at + wide, PROJ)
        proj_s[:, at:upto] = dot(n_s[...], w_cols[:, at:upto])
    sums[...] = jnp.zeros_like(sums)

    @pl.loop(0, 4)
    def _(i):
        at = pl.ds(pl.multiple_of(i * length, length), length)
        block_middle(
            proj_s[at, :],
            gh_s[at, :],
            bias[...],
            cosine[at, :],
            sine[at, :],
            segc[at, :],
            segr[i],
            ah_s,
            gp_s,
            sums,
            at,
        )

    for held, out in ((ah_s, ah_out), (gp_s, gp_out)):
        drains.append(pltpu.make_async_copy(held, out, out_sem.at[len(drains)]))
        drains[-1].start()

    @pl.loop(0, D // wide)
    def _(j):
        at = pl.ds(pl.multiple_of(j * wide, wide), wide)
        part = dot(gp_s[...], w_cols[at, :], BY_LAST)
        far_s[0, :, at] = part[near:].astype(LOW)
        near_s[0, :, at] = part[:near]

    for held, out in ((far_s, far_out), (near_s, near_out)):
        drains.append(pltpu.make_async_copy(held.at[0], out.at[0], out_sem.at[len(drains)]))
        drains[-1].start()

    @pl.loop(0, D // wide)
    def _(j):
        at = pl.ds(pl.multiple_of(j * wide, wide), wide)
        part = dot(ah_s[...], w_pair[:, at]) + tail[:, at]
        far_s[1, :, at] = part[near:].astype(LOW)
        near_s[1, :, at] = part[:near]

    for held, out in ((far_s, far_out), (near_s, near_out)):
        drains.append(pltpu.make_async_copy(held.at[1], out.at[1], out_sem.at[len(drains)]))
        drains[-1].start()
    for one in drains:
        one.wait()


def run_chunk(n_parts, g_parts, w_cols, w_pair, bias, tail, cosine, sine, segc, segr):
    length = n_parts[0].shape[0]
    rows = 4 * length
    near = rows // 2
    anywhere = pl.BlockSpec(memory_space=pl.ANY)
    here = pl.BlockSpec(memory_space=pltpu.VMEM)

    def shape(r, w, kind):
        return jax.ShapeDtypeStruct((r, w), kind)

    return pl.pallas_call(
        chunk_kernel,
        in_specs=[anywhere] * 8 + [here] * 8,
        out_specs=[anywhere] * 6 + [here],
        out_shape=[
            shape(rows, D, LOW),
            shape(rows, D, LOW),
            shape(rows, PAIR, LOW),
            shape(rows, PROJ, LOW),
            jax.ShapeDtypeStruct((2, near, D), LOW),
            jax.ShapeDtypeStruct((2, near, D), F32),
            shape(1, PROJ, F32),
        ],
        scratch_shapes=[
            pltpu.VMEM((rows, D), LOW),
            pltpu.VMEM((rows, D), LOW),
            pltpu.VMEM((rows, PAIR), F32),
            pltpu.VMEM((rows, PROJ), F32),
            pltpu.VMEM((rows, PAIR), LOW),
            pltpu.VMEM((rows, PROJ), LOW),
            pltpu.VMEM((2, near, D), LOW),
            pltpu.VMEM((2, near, D), F32),
            pltpu.SemaphoreType.DMA((2, 4)),
            pltpu.SemaphoreType.DMA((8,)),
        ],
        compiler_params=pltpu.CompilerParams(vmem_limit_bytes=44 * 2**20),
        cost_estimate=pl.CostEstimate(
            flops=4 * rows * D * (PROJ + PAIR) + 100 * rows * PROJ,
            bytes_accessed=rows * D * 16 + 4 * D * (PROJ + PAIR),
            transcendentals=rows * (2 * length + FCOL),
        ),
        name="chunk",
    )(*n_parts, *g_parts, w_cols, w_pair, bias, tail, cosine, sine, segc, segr)


def ranks_first(w_in, place, part):
    step = 16
    half = RANKS // 2

    def kernel(place_ref, w_ref, *outs):
        def put(rank, ref, at):
            for m in range(3):
                ref[at, :, m * QCOL : (m + 1) * QCOL] = w_ref[
                    :, m * D + rank * QCOL : m * D + (rank + 1) * QCOL
                ].astype(LOW)
            ref[at, :, 3 * QCOL :] = w_ref[
                :, 3 * D + rank * FCOL : 3 * D + (rank + 1) * FCOL
            ].astype(LOW)

        for rank in range(RANKS):
            put(rank, outs[-1], place_ref[rank])

        for n in range(NZ):
            outs[n][...] = outs[-1][2 * n : 2 * n + 2]
        outs[NZ][...] = outs[-1][half:]

    def block(count):
        return pl.BlockSpec((count, step, PROJ), lambda i, at: (0, i, 0))

    return pl.pallas_call(
        kernel,
        grid_spec=pltpu.PrefetchScalarGridSpec(
            num_scalar_prefetch=1,
            grid=(part // step,),
            in_specs=[
                pl.BlockSpec(
                    (step, 3 * D + FF), lambda i, at: (at[RANKS] * (part // step) + i, 0)
                )
            ],
            out_specs=[block(2)] * NZ + [block(half)],
            scratch_shapes=[pltpu.VMEM((RANKS, step, PROJ), LOW)],
        ),
        out_shape=[jax.ShapeDtypeStruct((2, part, PROJ), LOW)] * NZ
        + [jax.ShapeDtypeStruct((half, part, PROJ), LOW)],
        cost_estimate=pl.CostEstimate(
            flops=RANKS * part * PROJ, bytes_accessed=6 * RANKS * part * PROJ, transcendentals=0
        ),
        name="ranks_first",
    )(place, w_in)


def rows_home(pieces, place, part):
    each = pieces[0].shape[0]

    def kernel(place_ref, *refs):
        for i in range(2 * RANKS):
            at = pl.multiple_of(place_ref[i] * part, part)
            refs[-1][pl.ds(at, part), :] = refs[i // each][i % each]

    return pl.pallas_call(
        kernel,
        grid_spec=pltpu.PrefetchScalarGridSpec(
            num_scalar_prefetch=1,
            grid=(1,),
            in_specs=[pl.BlockSpec((each, part, PROJ), lambda i, at: (0, 0, 0))] * len(pieces),
            out_specs=pl.BlockSpec((D, PROJ), lambda i, at: (0, 0)),
        ),
        out_shape=jax.ShapeDtypeStruct((D, PROJ), LOW),
        cost_estimate=pl.CostEstimate(flops=0, bytes_accessed=4 * D * PROJ, transcendentals=0),
        name="rows_home",
    )(place, *pieces)


def split_sum(grads, held, place, part, first, blocks, kind):
    def kernel(place_ref, *refs):
        total = refs[0][...]
        for ref in refs[1 : len(grads)]:
            total = total + ref[...]
        copy = place_ref[RANKS]

        def give(sent, kept):
            refs[-2][...] = sent.astype(kind)
            for ref in refs[len(grads) : -2]:
                kept = kept + ref[...]
            refs[-1][...] = kept

        @pl.when(copy == 0)
        def _():
            give(total[:, 1], total[:, 0])

        @pl.when(copy != 0)
        def _():
            give(total[:, 0], total[:, 1])

    own = pl.BlockSpec((1, 2, part, PROJ), lambda i, at: (at[first + i], 0, 0, 0))
    old = pl.BlockSpec((1, part, PROJ), lambda i, at: (first + i, 0, 0))
    half = pl.BlockSpec((1, part, PROJ), lambda i, at: (i, 0, 0))
    return pl.pallas_call(
        kernel,
        grid_spec=pltpu.PrefetchScalarGridSpec(
            num_scalar_prefetch=1,
            grid=(blocks,),
            in_specs=[own] * len(grads) + [old] * len(held),
            out_specs=[half, half],
        ),
        out_shape=[
            jax.ShapeDtypeStruct((blocks, part, PROJ), kind),
            jax.ShapeDtypeStruct((blocks, part, PROJ), F32),
        ],
        cost_estimate=pl.CostEstimate(
            flops=8 * blocks * part * PROJ,
            bytes_accessed=30 * blocks * part * PROJ,
            transcendentals=0,
        ),
        name="split_sum",
    )(place, *[g.reshape(RANKS, 2, part, PROJ) for g in grads], *held)


def adamw_rows(weight, first, second, grads, slots, before=None):
    rows, cols = weight.shape
    part = rows // 2
    wide = D
    steps = cols // wide

    def kernel(slots_ref, w_ref, m_ref, v_ref, grads_ref, *refs):
        g_out, w_out, m_out, v_out = refs[-5:-1]
        grad_s = refs[-1]
        j = pl.program_id(0)

        @pl.when(j < 3)
        def _():
            at = pl.ds(pl.multiple_of(j * QCOL, QCOL), QCOL)
            for rank in range(RANKS):
                grad_s[:, rank * QCOL : (rank + 1) * QCOL] = grads_ref[
                    slots_ref[rank], :, at
                ].astype(F32)

        @pl.when(j >= 3)
        def _():
            per = D // FCOL
            for m in range(per):
                grad_s[:, m * FCOL : (m + 1) * FCOL] = grads_ref[
                    slots_ref[per * (j - 3) + m], :, 3 * QCOL :
                ].astype(F32)

        grad = grad_s[...]
        new_w, new_m, new_v = adamw(w_ref[...], grad, m_ref[...], v_ref[...], DECAY)
        g_out[...] = grad
        w_out[...] = new_w
        m_out[...] = new_m
        v_out[...] = new_v

    slab = pl.BlockSpec((part, wide), lambda j, at: (at[RANKS], j))
    held = [] if before is None else list(before)
    return pl.pallas_call(
        kernel,
        grid_spec=pltpu.PrefetchScalarGridSpec(
            num_scalar_prefetch=1,
            grid=(steps,),
            in_specs=[slab] * 3
            + [pl.BlockSpec((RANKS, part, PROJ), lambda j, at: (0, 0, 0))]
            + [pl.BlockSpec(memory_space=pl.ANY)] * len(held),
            out_specs=[slab] * 4,
            scratch_shapes=[pltpu.VMEM((part, wide), F32)],
        ),
        out_shape=[jax.ShapeDtypeStruct((rows, cols), F32)] * 4,
        input_output_aliases={5 + i: i for i in range(len(held))},
        cost_estimate=pl.CostEstimate(
            flops=20 * part * cols, bytes_accessed=30 * part * cols, transcendentals=part * cols
        ),
        name="adamw_rows",
    )(slots, weight, first, second, grads, *held)


def make_on_device(mesh):
    shards = mesh.shape["shard"]
    copies = mesh.shape["replica"]
    fold = shards // RANKS
    rank_of = lambda z, y, c: (z * 2 + y) * 2 + c

    def moves(target):
        pairs = []
        for z in range(NZ):
            for y in range(2):
                for c in range(2):
                    to = rank_of(*target(z, y, c))
                    for f in range(fold):
                        pairs.append((rank_of(z, y, c) * fold + f, to * fold + f))
        return pairs

    swap_core = moves(lambda z, y, c: (z, y, 1 - c))
    swap_y = moves(lambda z, y, c: (z, 1 - y, c))
    up_z = [moves(lambda z, y, c, n=n: ((z + n) % NZ, y, c)) for n in range(NZ)]

    def core(x):
        return lax.ppermute(x, "shard", swap_core)

    def across_y(x):
        return lax.ppermute(x, "shard", swap_y)

    def along_z(x, n):
        return lax.ppermute(x, "shard", up_z[n % NZ])

    def across_fold(x, n):
        return lax.ppermute(
            x,
            "shard",
            [(r * fold + f, r * fold + (f + n) % fold) for r in range(RANKS) for f in range(fold)],
        )

    def next_copy(x, n):
        return lax.ppermute(x, "replica", [(i, (i + n) % copies) for i in range(copies)])

    def fold_gather(x, f):
        if fold == 1:
            return x
        parts = jnp.stack([x] + [across_fold(x, n) for n in range(1, fold)])
        order = (f - jnp.arange(fold)) % fold
        return jnp.take(parts, order, axis=0).reshape((fold * x.shape[0],) + x.shape[1:])

    def fold_scatter(x, f):
        if fold == 1:
            return x
        parts = x.reshape((fold, x.shape[0] // fold) + x.shape[1:])
        total = lax.dynamic_index_in_dim(parts, f, 0, keepdims=False)
        for n in range(1, fold):
            part = lax.dynamic_index_in_dim(parts, (f + n) % fold, 0, keepdims=False)
            total = total + across_fold(part, n).astype(F32)
        return total

    def gather_z(x):
        above = along_z(x, 3)
        below = along_z(x, 1)
        opposite = along_z(above, 3)
        chunks = []
        for x in (x, below, opposite, above):
            flipped = across_y(x)
            far = core(x)
            chunks.append((x, flipped, far, core(flipped)))
        return chunks

    def table(me, entries):
        rows = [
            entries(r // 4, r // 2 % 2, r % 2) for r in range(RANKS) for _ in range(fold)
        ]
        return lax.dynamic_index_in_dim(jnp.array(rows, dtype=jnp.int32), me, 0, keepdims=False)

    def near(z, y, c, n, dy, dc):
        return rank_of((z + n) % NZ, (y + dy) % 2, (c + dc) % 2)

    def columns_of(w_in, me, z, y, c, f, copy):
        rows = w_in.shape[0] * fold
        part = rows // copies
        if fold == 1 and copies == 2:
            def slots(z, y, c):
                order = [near(z, y, c, n, i, j) for j in (0, 1) for n in range(NZ) for i in (0, 1)]
                return [order.index(r) for r in range(RANKS)]

            place = jnp.concatenate([table(me, slots), copy.reshape(1)])
            *kept, sent = ranks_first(w_in, place, part)
            came = core(sent).reshape(NZ, 2, part, PROJ)
            pieces = []
            for n in (0, 2, 1, 3):
                piece = jnp.stack([kept[n], came[n]], axis=1)
                if n:
                    piece = along_z(piece, n)
                over = across_y(piece[1])
                piece = jnp.concatenate([piece[0], over])
                pieces.append((piece, next_copy(piece, 1)))
            home = table(
                me,
                lambda z, y, c: [
                    2 * near(z, y, c, -n, i, j) for n in (0, 2, 1, 3) for i in (0, 1) for j in (0, 1)
                ],
            )
            home = jnp.concatenate([home + copy, home + (1 - copy)])
            return rows_home([p[0] for p in pieces] + [p[1] for p in pieces], home, part)
        low_in = fold_gather(w_in.astype(LOW), f)
        by_rank = jnp.concatenate(
            [
                low_in[:, :D].reshape(rows, RANKS, QCOL),
                low_in[:, D : 2 * D].reshape(rows, RANKS, QCOL),
                low_in[:, 2 * D : 3 * D].reshape(rows, RANKS, QCOL),
                low_in[:, 3 * D :].reshape(rows, RANKS, FCOL),
            ],
            axis=2,
        )
        turned = by_rank.transpose(1, 0, 2).reshape(NZ, 2, 2, rows, PROJ)
        return to_ranks(turned, z, y, c).reshape(D, PROJ)

    def to_ranks(blocks, z, y, c):
        kept = lax.dynamic_index_in_dim(blocks, c, 2, keepdims=False)
        came = core(lax.dynamic_index_in_dim(blocks, 1 - c, 2, keepdims=False))
        blocks = jnp.stack([jnp.where(c == 0, kept, came), jnp.where(c == 0, came, kept)], axis=2)
        kept = lax.dynamic_index_in_dim(blocks, y, 1, keepdims=False)
        came = across_y(lax.dynamic_index_in_dim(blocks, 1 - y, 1, keepdims=False))
        blocks = jnp.stack([jnp.where(y == 0, kept, came), jnp.where(y == 0, came, kept)], axis=1)
        by_z = [lax.dynamic_index_in_dim(blocks, z, 0, keepdims=False)]
        for n in range(1, NZ):
            by_z.append(
                along_z(lax.dynamic_index_in_dim(blocks, (z + n) % NZ, 0, keepdims=False), n)
            )
        return jnp.take(jnp.stack(by_z), (z - jnp.arange(NZ)) % NZ, axis=0)

    def start_in(grad_in, me, copy):
        part = D // RANKS // 2
        place = table(
            me,
            lambda z, y, c: [near(z, y, c, n, i, j) for n in GRAD_ORDER for i in (0, 1) for j in (0, 1)],
        )
        place = jnp.concatenate([place, copy.reshape(1)])
        sent, kept = split_sum(grad_in, (), place, part, 0, RANKS, F32)
        return place, kept, next_copy(sent, 1)

    def finish_in(grad_in, early, w_in, m_in, v_in, me, z, y, c, f, copy):
        rows = w_in.shape[0] * fold
        part = rows // copies
        if fold == 1 and copies == 2:
            place, kept, heard = early
            halves = []
            for i, n in enumerate(GRAD_ORDER):
                sent, base = split_sum(
                    grad_in[EARLY:], (kept, heard), place, part, 4 * i, 4, LOW
                )
                late = next_copy(sent, 1)
                block = (base + late).astype(LOW)
                if n:
                    block = along_z(block, n)
                came = across_y(block[2:])
                block = jnp.stack([block[:2], came])
                came = core(block[:, 1])
                block = jnp.stack([block[:, 0], came], axis=1)
                block = block.reshape(4, part, PROJ)
                came = next_copy(block, 1)
                halves.append((block, came))
            own = jnp.concatenate([h[0] for h in halves])
            other = jnp.concatenate([h[1] for h in halves])

            def slots(z, y, c):
                order = [near(z, y, c, -n, i, j) for n in GRAD_ORDER for i in (0, 1) for j in (0, 1)]
                return [order.index(r) for r in range(RANKS)]

            slot = table(me, slots)
            mine = jnp.concatenate([slot, copy.reshape(1)])
            theirs = jnp.concatenate([slot, 1 - copy.reshape(1)])
            first = adamw_rows(w_in, m_in, v_in, own, mine)
            return adamw_rows(w_in, m_in, v_in, other, theirs, first)
        grad_in = sum(grad_in[1:], grad_in[0])
        back = to_ranks(grad_in.astype(LOW).reshape(NZ, 2, 2, rows, PROJ), z, y, c)
        both = back.reshape(RANKS, rows, PROJ).transpose(1, 0, 2)
        both = jnp.concatenate(
            [
                both[:, :, :QCOL].reshape(rows, D),
                both[:, :, QCOL : 2 * QCOL].reshape(rows, D),
                both[:, :, 2 * QCOL : 3 * QCOL].reshape(rows, D),
                both[:, :, 3 * QCOL :].reshape(rows, FF),
            ],
            axis=1,
        )
        grad = fold_scatter(both, f).astype(F32)
        for moved in [next_copy(grad, n) for n in range(1, copies)]:
            grad = grad + moved
        return (grad,) + adamw(w_in, grad, m_in, v_in, DECAY)

    def on_device(
        tokens,
        seg_ids,
        cotangent,
        w_in,
        w_out,
        w_fc2,
        vectors,
        m_in,
        v_in,
        m_out,
        v_out,
        m_fc2,
        v_fc2,
        m_vec,
        v_vec,
    ):
        length = tokens.shape[0]
        me = lax.axis_index("shard")
        copy = lax.axis_index("replica")
        t = me // fold
        f = me % fold
        z, y, c = t // 4, (t // 2) % 2, t % 2

        g_chunks = gather_z(cotangent)

        w_cols = columns_of(w_in, me, z, y, c, f, copy)
        w_pair = jnp.concatenate(
            [fold_gather(w_out.astype(LOW), f), fold_gather(w_fc2.astype(LOW), f)], axis=0
        )

        order = jnp.arange(length, dtype=jnp.int32)
        same = seg_ids[:, None] == seg_ids[None, :]
        place = jnp.sum((same & (order[None, :] < order[:, None])).astype(F32), axis=1)
        grouped = fold_gather(vectors.reshape(-1, 11), f)
        small = jnp.concatenate([grouped[:, 9], grouped[:, 10], seg_ids.astype(F32), place])
        small = small.reshape(1, -1)
        heard = [small]
        for n in range(1, NZ):
            heard.append(along_z(small, n))
        small = jnp.concatenate(heard, axis=0)
        small = jnp.stack([small, across_y(small)], axis=1)
        small = jnp.stack([small, core(small)], axis=2)
        gains = small[..., : 2 * QCOL]
        gains = jnp.take(gains, (z - jnp.arange(NZ)) % NZ, axis=0)
        gains = jnp.where(y == 0, gains, gains[:, ::-1])
        gains = jnp.where(c == 0, gains, gains[:, :, ::-1]).reshape(RANKS, 2, QCOL)
        gain = gains[:, 0].reshape(D)
        shift = gains[:, 1].reshape(D)
        tail = small[..., 2 * QCOL :].transpose(0, 2, 1, 3).reshape(NZ, 4, 2, length)
        segs = tail[:, :, 0]
        places = tail[:, :, 1]
        lane = jnp.arange(QCOL, dtype=jnp.int32) % HEAD
        freqs = 10000.0 ** (-(lane % (ROT // 2)).astype(F32) * (2.0 / ROT))
        freqs = jnp.where(lane < ROT, freqs, 0.0)
        inputs = tokens.astype(F32)
        centred = inputs - jnp.mean(inputs, axis=1, keepdims=True)
        inv_std = lax.rsqrt(jnp.mean(centred * centred, axis=1, keepdims=True) + NORM_EPS)
        standard = centred * inv_std
        normed = (standard * gain + shift).astype(LOW)
        n_chunks = gather_z(normed)

        bias_in = jnp.concatenate(
            [grouped[:, 0], grouped[:, 1], grouped[:, 2], grouped[:, 3:7].reshape(FCOL)]
        ).reshape(1, PROJ)
        bias_tail = lax.dynamic_update_slice(
            jnp.zeros((D,), F32), grouped[:, 7] + grouped[:, 8], (t * QCOL,)
        )

        def scatter_add(near, far, n, carried):
            came = core(far)
            sent = (near[:, length:] + came[:, length:].astype(F32)).astype(LOW)
            over = across_y(sent)
            own = near[:, :length] + came[:, :length].astype(F32) + over.astype(F32)
            if carried is not None:
                own = own + carried
            if n == 0:
                return own
            return along_z(own.astype(LOW), 1 if n == 3 else 3).astype(F32)

        totals = []
        early = None
        grad_in = []
        grad_pair = []
        proj_sum = []
        for n in CHUNKS:
            gc = g_chunks[n]
            nc = n_chunks[n]
            if grad_in:
                gc, nc, last_in, last_pair = lax.optimization_barrier(
                    (gc, nc, grad_in[-1], grad_pair[-1])
                )
                grad_in[-1] = last_in
                grad_pair[-1] = last_pair
            angles = places[n].reshape(4 * length, 1) * freqs
            n_cat, g_cat, ah, gp, far, near, sums = run_chunk(
                nc,
                gc,
                w_cols,
                w_pair,
                bias_in,
                bias_tail.reshape(1, D),
                jnp.cos(angles),
                jnp.sin(angles),
                segs[n].reshape(4 * length, 1),
                segs[n].reshape(4, 1, length),
            )
            grad_in.append(dot(n_cat, gp, BY_FIRST))
            grad_pair.append(dot(ah, g_cat, BY_FIRST))
            proj_sum.append(sums)
            carried = scatter_add(near, far, n, totals.pop() if n == 1 else None)
            totals.append(carried)
            if len(grad_in) == EARLY and fold == 1 and copies == 2:
                early = start_in(grad_in, me, copy)
        gn_total = sum([part[0] for part in totals[1:]], totals[0][0])
        out_total = sum([part[1] for part in totals[1:]], totals[0][1])
        proj_sum = sum(proj_sum[1:], proj_sum[0])
        grad_pair = sum(grad_pair[1:], grad_pair[0])

        output = (inputs + out_total).astype(LOW)
        upstream = cotangent.astype(F32)
        scaled = gn_total * gain
        grad_tokens = upstream + inv_std * (
            scaled
            - jnp.mean(scaled, axis=1, keepdims=True)
            - standard * jnp.mean(scaled * standard, axis=1, keepdims=True)
        )

        sums = jnp.stack(
            [jnp.sum(upstream, axis=0), jnp.sum(gn_total * standard, axis=0), jnp.sum(gn_total, axis=0)]
        )
        sums = sums + core(sums)
        sums = sums + across_y(sums)
        for moved in [along_z(sums, n) for n in range(1, NZ)]:
            sums = sums + moved
        sums = lax.dynamic_slice(sums, (0, t * QCOL), (3, QCOL))
        vec = jnp.concatenate(
            [
                proj_sum[0, : 3 * QCOL].reshape(3, QCOL).T,
                proj_sum[0, 3 * QCOL :].reshape(QCOL, 4),
                sums[0][:, None],
                sums[0][:, None],
                sums[1][:, None],
                sums[2][:, None],
            ],
            axis=1,
        )
        vec = fold_scatter(vec, f).reshape(-1)
        for moved in [next_copy(vec, n) for n in range(1, copies)]:
            vec = vec + moved

        g_out = fold_scatter(grad_pair[:QCOL], f)
        g_fc2 = fold_scatter(grad_pair[QCOL:], f)
        g_pair = jnp.concatenate([g_out, g_fc2], axis=0).astype(LOW)
        pair_total = g_pair.astype(F32)
        for n in range(1, copies):
            pair_total = pair_total + next_copy(g_pair, n).astype(F32)
        grad_out = pair_total[: g_out.shape[0]]
        grad_fc2 = pair_total[g_out.shape[0] :]

        grad_w_in, new_in, new_m_in, new_v_in = finish_in(
            grad_in, early, w_in, m_in, v_in, me, z, y, c, f, copy
        )
        new_out, new_m_out, new_v_out = adamw(w_out, grad_out, m_out, v_out, DECAY)
        new_fc2, new_m_fc2, new_v_fc2 = adamw(w_fc2, grad_fc2, m_fc2, v_fc2, DECAY)
        new_vec, new_m_vec, new_v_vec = adamw(vectors, vec, m_vec, v_vec, 0.0)
        return (
            output,
            grad_tokens,
            grad_w_in,
            grad_out,
            grad_fc2,
            vec,
            new_in,
            new_out,
            new_fc2,
            new_vec,
            new_m_in,
            new_v_in,
            new_m_out,
            new_v_out,
            new_m_fc2,
            new_v_fc2,
            new_m_vec,
            new_v_vec,
        )

    return on_device


def solution(mesh):
    both = P(("replica", "shard"), None)
    flat = P("shard")
    rows = P("shard", None)
    return jax.shard_map(
        make_on_device(mesh),
        mesh=mesh,
        in_specs=(both, P(("replica", "shard")), both, rows, rows, rows, flat)
        + (rows,) * 6
        + (flat, flat),
        out_specs=(both, both, rows, rows, rows, flat)
        + (rows, rows, rows, flat)
        + (rows,) * 6
        + (flat, flat),
        check_vma=False,
    )
```

profile of v0, /device:TPU:0, one launch (start us, length us, event | category | flops | bytes accessed | tf_op | source)
XLA Modules:
  0.0 801.9 jit_solution(995318384862331457)
XLA Ops:
  3.6 5.1 collective-permute-start.2
  18.9 4.9 ranks_first.1
  24.5 6.8 collective-permute-done.3
  37.6 5.4 collective-permute-done.12
  45.3 21.6 %collective-permute-done.13 = bf16[2,2,64,896]{3,2,0,1:T(8,128)(2,1)S(1)} collective-permute-done((bf16[2,2,64,896]{3,2,0,1:T(8,128)(2,1)S(1)}, bf16[2,2,64,896]{3,2,0,1:T(8,128)(2,1)S(1)}, u32[]{:S(2)}, u32[]{:S(2)}) %collective-permute-start.13) | collective-permute-done | bytes 458784 | tf_op jit(solution)/shard_map/ppermute | solution.py:437
  68.5 10.8 %collective-permute-done.17 = bf16[2,2,64,896]{3,2,1,0:T(8,128)(2,1)S(1)} collective-permute-done((bf16[2,2,64,896]{3,2,1,0:T(8,128)(2,1)S(1)}, bf16[2,2,64,896]{3,2,1,0:T(8,128)(2,1)S(1)}, u32[]{:S(2)}, u32[]{:S(2)}) %collective-permute-start.17) | collective-permute-done | bytes 458784 | tf_op jit(solution)/shard_map/ppermute | solution.py:437
  82.3 5.5 collective-permute-done.16
  103.6 7.7 collective-permute-done.20.refs_5_
  111.3 9.8 %collective-permute-done.21.refs_6_ = bf16[4,64,896]{2,1,0:T(8,128)(2,1)} collective-permute-done((bf16[4,64,896]{2,1,0:T(8,128)(2,1)}, bf16[4,64,896]{2,1,0:T(8,128)(2,1)}, u32[]{:S(2)}, u32[]{:S(2)}) %collective-permute-start.21) | collective-permute-done | bytes 458784 | tf_op jit(solution)/shard_map/ppermute | solution.py:447
  121.2 5.4 collective-permute-done.22.refs_7_
  132.9 7.8 multiply_sine_fusion
  140.8 4.8 rows_home.1.w_cols
  145.6 4.3 collective-permute-start.44
  155.3 28.1 %chunk.4 = (bf16[768,2048]{1,0:T(8,128)(2,1)}, bf16[768,2048]{1,0:T(8,128)(2,1)}, bf16[768,640]{1,0:T(8,128)(2,1)S(1)}, bf16[768,896]{1,0:T(8,128)(2,1)S(1)}, bf...) custom-call(bf16[192,2048]{1,0:T(8,128)(2,1)S(1)} %fusion.8.n_own, ...), custom_call_target="tpu_custom_call" | custom-call | flops 9732489216 | bytes 37748736 | tf_op jit(solution)/shard_map/chunk/pallas_call | solution.py:206
  184.6 25.6 %collective-permute-start.48 = (bf16[192,2048]{1,0:T(8,128)(2,1)}, bf16[192,2048]{1,0:T(8,128)(2,1)S(1)}, u32[]{:S(2)}, u32[]{:S(2)}) collective-permute-start(bf16[192,2048]{1,0:T(8,128)(2,1)} %collective-permute-done.29.n_own), channel_id=1, source_target_pairs={{0,12},{1,13},{2,14},{3,15},{4,0},{5,1},{6,2},{7,3},{8,4},{9,5},{1... | collective-permute-start | bytes 2359304 | tf_op jit(solution)/shard_map/ppermute | solution.py:437
  210.8 6.6 fusion.60
  217.5 5.8 fusion.59
  227.4 26.9 %chunk.5 = (bf16[768,2048]{1,0:T(8,128)(2,1)}, bf16[768,2048]{1,0:T(8,128)(2,1)}, bf16[768,640]{1,0:T(8,128)(2,1)S(1)}, bf16[768,896]{1,0:T(8,128)(2,1)S(1)}, bf...) custom-call(bf16[192,2048]{1,0:T(8,128)(2,1)} %collective-permute-done.29.n_own, ...), custom_call_target="tpu_custom_call" | custom-call | flops 9732489216 | bytes 37748736 | tf_op jit(solution)/shard_map/chunk/pallas_call | solution.py:206
  254.3 23.0 %collective-permute-done.45.g_y = bf16[192,2048]{1,0:T(8,128)(2,1)S(1)} collective-permute-done((bf16[192,2048]{1,0:T(8,128)(2,1)S(1)}, bf16[192,2048]{1,0:T(8,128)(2,1)S(1)}, u32[]{:S(2)}, u32[]{:S(2)}) %collective-permute-start.45) | collective-permute-done | bytes 786464 | tf_op jit(solution)/shard_map/ppermute | solution.py:434
  277.4 16.3 %collective-permute-done.49.n_y = bf16[192,2048]{1,0:T(8,128)(2,1)S(1)} collective-permute-done((bf16[192,2048]{1,0:T(8,128)(2,1)S(1)}, bf16[192,2048]{1,0:T(8,128)(2,1)S(1)}, u32[]{:S(2)}, u32[]{:S(2)}) %collective-permute-start.49) | collective-permute-done | bytes 786464 | tf_op jit(solution)/shard_map/ppermute | solution.py:434
  293.7 6.7 fusion.62
  300.4 5.6 fusion.61
  307.5 27.1 %chunk.6 = (bf16[768,2048]{1,0:T(8,128)(2,1)}, bf16[768,2048]{1,0:T(8,128)(2,1)}, bf16[768,640]{1,0:T(8,128)(2,1)S(1)}, bf16[768,896]{1,0:T(8,128)(2,1)S(1)}, bf...) custom-call(bf16[192,2048]{1,0:T(8,128)(2,1)S(1)} %collective-permute-done.48.n_own, ...), custom_call_target="tpu_custom_call" | custom-call | flops 9732489216 | bytes 37748736 | tf_op jit(solution)/shard_map/chunk/pallas_call | solution.py:206
  334.6 6.6 fusion.64
  341.2 5.6 fusion.63
  346.8 27.3 %chunk.7 = (bf16[768,2048]{1,0:T(8,128)(2,1)}, bf16[768,2048]{1,0:T(8,128)(2,1)}, bf16[768,640]{1,0:T(8,128)(2,1)S(1)}, bf16[768,896]{1,0:T(8,128)(2,1)S(1)}, bf...) custom-call(bf16[192,2048]{1,0:T(8,128)(2,1)S(1)} %collective-permute-done.40.n_own, ...), custom_call_target="tpu_custom_call" | custom-call | flops 9732489216 | bytes 37748736 | tf_op jit(solution)/shard_map/chunk/pallas_call | solution.py:206
  375.2 6.4 fusion.66
  381.6 10.5 %add_convert_fusion = bf16[640,2048]{1,0:T(8,128)(2,1)} fusion(f32[640,2048]{1,0:T(8,128)} %fusion.66, f32[640,2048]{1,0:T(8,128)} %fusion.64, f32[640,2048]{1,0:T(8,128)} %fusion.60, f32[640,2048]{1,0:T(8,128)} %fusion.62), kind=kLoop, calls=%fused_computation.3 | loop fusion | flops 5242880 | bytes 23592960 | tf_op jit(solution)/shard_map/convert_element_type | solution.py:753
  394.3 14.0 %split_sum.5 = (f32[16,64,896]{2,1,0:T(8,128)}, f32[16,64,896]{2,1,0:T(8,128)}) custom-call(s32[17]{0:T(128)} %get-tuple-element.280.place_ref, f32[16,2,64,896]{3,2,1,0:T(8,128)} %bitcast.153, f32[16,2,64,896]{3,2,1,0:T(8,128)} %bitcast.154), custom_call_target="tpu_custom_call" | custom-call | flops 7340032 | bytes 27525120 | tf_op jit(solution)/shard_map/split_sum/pallas_call | solution.py:333
  410.4 7.4 fusion.65
  420.8 4.2 add_convert_fusion.6
  426.5 25.7 %collective-permute-done.78 = bf16[640,2048]{1,0:T(8,128)(2,1)} collective-permute-done((bf16[640,2048]{1,0:T(8,128)(2,1)}, bf16[640,2048]{1,0:T(8,128)(2,1)}, u32[]{:S(2)}, u32[]{:S(2)}) %collective-permute-start.78) | collective-permute-done | bytes 2621472 | tf_op jit(solution)/shard_map/ppermute | solution.py:447
  460.1 6.7 multiply_subtract_fusion
  470.3 59.9 %collective-permute-done.58.refs_3_ = f32[16,64,896]{2,1,0:T(8,128)} collective-permute-done((f32[16,64,896]{2,1,0:T(8,128)}, f32[16,64,896]{2,1,0:T(8,128)}, u32[]{:S(2)}, u32[]{:S(2)}) %collective-permute-start.58) | collective-permute-done | bytes 3670048 | tf_op jit(solution)/shard_map/ppermute | solution.py:447
  530.2 5.0 split_sum.9
  536.7 5.0 split_sum.8
  542.3 5.0 split_sum.7
  547.3 5.0 split_sum.6
  559.2 4.0 add_convert_fusion.2
  563.4 5.1 collective-permute-done.64
  570.1 6.8 collective-permute-done.59
  578.5 52.5 %collective-permute-done.75 = bf16[2,64,896]{2,1,0:T(8,128)(2,1)S(1)} collective-permute-done((bf16[2,64,896]{2,1,0:T(8,128)(2,1)S(1)}, bf16[2,64,896]{2,1,0:T(8,128)(2,1)S(1)}, u32[]{:S(2)}, u32[]{:S(2)}) %collective-permute-start.75) | collective-permute-done | bytes 229408 | tf_op jit(solution)/shard_map/ppermute | solution.py:434
  631.0 3.9 collective-permute-start.65
  648.6 7.5 collective-permute-done.65
  657.6 78.9 %collective-permute-done.60 = bf16[4,64,896]{2,1,0:T(8,128)(2,1)S(1)} collective-permute-done((bf16[4,64,896]{2,1,0:T(8,128)(2,1)S(1)}, bf16[4,64,896]{2,1,0:T(8,128)(2,1)S(1)}, u32[]{:S(2)}, u32[]{:S(2)}) %collective-permute-start.60) | collective-permute-done | bytes 458784 | tf_op jit(solution)/shard_map/ppermute | solution.py:437
  738.7 4.7 collective-permute-done.66
  767.2 13.8 %adamw_rows.2 = (f32[128,14336]{1,0:T(8,128)}, f32[128,14336]{1,0:T(8,128)}, f32[128,14336]{1,0:T(8,128)}, f32[128,14336]{1,0:T(8,128)}) custom-call(s32[17]{0:T(128)} %get-tuple-element.271.slots_ref, f32[128,14336]{1,0:T(8,128)} %w_ref.5, f32[128,14336]{1,0:T(8,128)} %m_ref.3, f32[128,14336]{1,0:T(8,128)} %v_ref.3, ...), custom_call_target="tpu_custom_call" | custom-call | flops 18350080 | bytes 27525120 | tf_op jit(solution)/shard_map/adamw_rows/pallas_call | solution.py:390
  787.2 13.8 %adamw_rows.3 = (f32[128,14336]{1,0:T(8,128)}, f32[128,14336]{1,0:T(8,128)}, f32[128,14336]{1,0:T(8,128)}, f32[128,14336]{1,0:T(8,128)}) custom-call(s32[17]{0:T(128)} %get-tuple-element.272.slots_ref, f32[128,14336]{1,0:T(8,128)} %w_ref.5, f32[128,14336]{1,0:T(8,128)} %m_ref.3, ...), custom_call_target="tpu_custom_call", output_to_operand_aliasing={{0}: (5, {}), {1}: (6, {}), {2}: (7, {}), {3}: (8, {})} | custom-call | flops 18350080 | bytes 27525120 | tf_op jit(solution)/shard_map/adamw_rows/pallas_call | solution.py:390
  (391 shorter events, 143.1 us)
Async XLA Ops:
  9.7 83.6 %collective-permute-start.25 = (bf16[192,2048]{1,0:T(8,128)(2,1)}, bf16[192,2048]{1,0:T(8,128)(2,1)S(1)}, u32[]{:S(2)}, u32[]{:S(2)}) collective-permute-start(bf16[192,2048]{1,0:T(8,128)(2,1)} %g_own.1), channel_id=1, source_target_pairs={{0,12},{1,13},{2,14},{3,15},{4,0},{5,1},{6,2},{7,3},{8,4},{9,5},{1... | collective-permute-start | bytes 2359304 | tf_op jit(solution)/shard_map/ppermute | solution.py:437
  12.5 81.3 %collective-permute-start.8 = (bf16[192,2048]{1,0:T(8,128)(2,1)}, bf16[192,2048]{1,0:T(8,128)(2,1)}, u32[]{:S(2)}, u32[]{:S(2)}) collective-permute-start(bf16[192,2048]{1,0:T(8,128)(2,1)} %g_own.1), channel_id=1, source_target_pairs={{0,2},{1,3},{2,0},{3,1},{4,6},{5,7},{6,4},{7,5},{8,10},{9,11},{10,... | collective-permute-start | bytes 2359304 | tf_op jit(solution)/shard_map/ppermute | solution.py:434
  34.6 32.3 %collective-permute-start.13 = (bf16[2,2,64,896]{3,2,0,1:T(8,128)(2,1)S(1)}, bf16[2,2,64,896]{3,2,0,1:T(8,128)(2,1)S(1)}, u32[]{:S(2)}, u32[]{:S(2)}) collective-permute-start(bf16[2,2,64,896]{3,2,0,1:T(8,128)(2,1)S(1)} %pad_maximum_fusion.4), channel_id=1, source_target_pairs={{0,8},{1,9},{2,10},{3,11},{4,12},{5,13},{6,14},{7,15},{8,0},{9,1},... | collective-permute-start | bytes 1376264 | tf_op jit(solution)/shard_map/ppermute | solution.py:437
  37.2 29.8 %collective-permute-start.15 = (bf16[2,2,64,896]{3,2,0,1:T(8,128)(2,1)S(1)}, bf16[2,2,64,896]{3,2,0,1:T(8,128)(2,1)S(1)}, u32[]{:S(2)}, u32[]{:S(2)}) collective-permute-start(bf16[2,2,64,896]{3,2,0,1:T(8,128)(2,1)S(1)} %pad_maximum_fusion.6), channel_id=1, source_target_pairs={{0,4},{1,5},{2,6},{3,7},{4,8},{5,9},{6,10},{7,11},{8,12},{9,13},{1... | collective-permute-start | bytes 1376264 | tf_op jit(solution)/shard_map/ppermute | solution.py:437
  43.0 58.0 %collective-permute-start.5 = (bf16[192,2048]{1,0:T(8,128)(2,1)S(1)}, bf16[192,2048]{1,0:T(8,128)(2,1)}, u32[]{:S(2)}, u32[]{:S(2)}) collective-permute-start(bf16[192,2048]{1,0:T(8,128)(2,1)S(1)} %fusion.8.n_own), channel_id=1, source_target_pairs={{0,2},{1,3},{2,0},{3,1},{4,6},{5,7},{6,4},{7,5},{8,10},{9,11},{10,... | collective-permute-start | bytes 2359304 | tf_op jit(solution)/shard_map/ppermute | solution.py:434
  93.3 27.9 %collective-permute-start.21 = (bf16[4,64,896]{2,1,0:T(8,128)(2,1)}, bf16[4,64,896]{2,1,0:T(8,128)(2,1)}, u32[]{:S(2)}, u32[]{:S(2)}) collective-permute-start(bf16[4,64,896]{2,1,0:T(8,128)(2,1)} %pad_maximum_fusion.7.refs_2_), channel_id=1, source_target_pairs={{0,16},{16,0},{1,17},{17,1},{2,18},{18,2},{3,19},{19,3},{4,20},{20... | collective-permute-start | bytes 1376264 | tf_op jit(solution)/shard_map/ppermute | solution.py:447
  93.8 32.8 %collective-permute-start.22 = (bf16[4,64,896]{2,1,0:T(8,128)(2,1)}, bf16[4,64,896]{2,1,0:T(8,128)(2,1)}, u32[]{:S(2)}, u32[]{:S(2)}) collective-permute-start(bf16[4,64,896]{2,1,0:T(8,128)(2,1)} %pad_maximum_fusion.9.refs_3_), channel_id=1, source_target_pairs={{0,16},{16,0},{1,17},{17,1},{2,18},{18,2},{3,19},{19,3},{4,20},{20... | collective-permute-start | bytes 1376264 | tf_op jit(solution)/shard_map/ppermute | solution.py:447
  101.0 44.5 %collective-permute-start.9 = (bf16[192,2048]{1,0:T(8,128)(2,1)S(1)}, bf16[192,2048]{1,0:T(8,128)(2,1)}, u32[]{:S(2)}, u32[]{:S(2)}) collective-permute-start(bf16[192,2048]{1,0:T(8,128)(2,1)S(1)} %copy-done), channel_id=1, source_target_pairs={{0,1},{1,0},{2,3},{3,2},{4,5},{5,4},{6,7},{7,6},{8,9},{9,8},{10,11... | collective-permute-start | bytes 2359304 | tf_op jit(solution)/shard_map/ppermute | solution.py:431
  101.5 44.0 %collective-permute-start.29 = (bf16[192,2048]{1,0:T(8,128)(2,1)S(1)}, bf16[192,2048]{1,0:T(8,128)(2,1)}, u32[]{:S(2)}, u32[]{:S(2)}) collective-permute-start(bf16[192,2048]{1,0:T(8,128)(2,1)S(1)} %fusion.8.n_own), channel_id=1, source_target_pairs={{0,12},{1,13},{2,14},{3,15},{4,0},{5,1},{6,2},{7,3},{8,4},{9,5},{1... | collective-permute-start | bytes 2359304 | tf_op jit(solution)/shard_map/ppermute | solution.py:437
  111.3 34.3 %collective-permute-start.6 = (bf16[192,2048]{1,0:T(8,128)(2,1)S(1)}, bf16[192,2048]{1,0:T(8,128)(2,1)}, u32[]{:S(2)}, u32[]{:S(2)}) collective-permute-start(bf16[192,2048]{1,0:T(8,128)(2,1)S(1)} %fusion.8.n_own), channel_id=1, source_target_pairs={{0,1},{1,0},{2,3},{3,2},{4,5},{5,4},{6,7},{7,6},{8,9},{9,8},{10,11... | collective-permute-start | bytes 2359304 | tf_op jit(solution)/shard_map/ppermute | solution.py:431
  121.2 28.7 %collective-permute-start.10 = (bf16[192,2048]{1,0:T(8,128)(2,1)}, bf16[192,2048]{1,0:T(8,128)(2,1)}, u32[]{:S(2)}, u32[]{:S(2)}) collective-permute-start(bf16[192,2048]{1,0:T(8,128)(2,1)} %collective-permute-done.8.g_y), channel_id=1, source_target_pairs={{0,1},{1,0},{2,3},{3,2},{4,5},{5,4},{6,7},{7,6},{8,9},{9,8},{10,11... | collective-permute-start | bytes 2359304 | tf_op jit(solution)/shard_map/ppermute | solution.py:431
  145.5 37.9 %collective-permute-start.36 = (bf16[192,2048]{1,0:T(8,128)(2,1)S(1)}, bf16[192,2048]{1,0:T(8,128)(2,1)S(1)}, u32[]{:S(2)}, u32[]{:S(2)}) collective-permute-start(bf16[192,2048]{1,0:T(8,128)(2,1)S(1)} %copy-done), channel_id=1, source_target_pairs={{0,4},{1,5},{2,6},{3,7},{4,8},{5,9},{6,10},{7,11},{8,12},{9,13},{1... | collective-permute-start | bytes 2359304 | tf_op jit(solution)/shard_map/ppermute | solution.py:437
  145.5 39.1 %collective-permute-start.40 = (bf16[192,2048]{1,0:T(8,128)(2,1)S(1)}, bf16[192,2048]{1,0:T(8,128)(2,1)S(1)}, u32[]{:S(2)}, u32[]{:S(2)}) collective-permute-start(bf16[192,2048]{1,0:T(8,128)(2,1)S(1)} %fusion.8.n_own), channel_id=1, source_target_pairs={{0,4},{1,5},{2,6},{3,7},{4,8},{5,9},{6,10},{7,11},{8,12},{9,13},{1... | collective-permute-start | bytes 2359304 | tf_op jit(solution)/shard_map/ppermute | solution.py:437
  145.6 64.6 %collective-permute-start.44 = (bf16[192,2048]{1,0:T(8,128)(2,1)}, bf16[192,2048]{1,0:T(8,128)(2,1)S(1)}, u32[]{:S(2)}, u32[]{:S(2)}) collective-permute-start(bf16[192,2048]{1,0:T(8,128)(2,1)} %copy-done.14), channel_id=1, source_target_pairs={{0,12},{1,13},{2,14},{3,15},{4,0},{5,1},{6,2},{7,3},{8,4},{9,5},{1... | collective-permute-start | bytes 2359304 | tf_op jit(solution)/shard_map/ppermute | solution.py:437
  149.9 60.4 %collective-permute-start.26 = (bf16[192,2048]{1,0:T(8,128)(2,1)}, bf16[192,2048]{1,0:T(8,128)(2,1)S(1)}, u32[]{:S(2)}, u32[]{:S(2)}) collective-permute-start(bf16[192,2048]{1,0:T(8,128)(2,1)} %copy-done.14), channel_id=1, source_target_pairs={{0,2},{1,3},{2,0},{3,1},{4,6},{5,7},{6,4},{7,5},{8,10},{9,11},{10,... | collective-permute-start | bytes 2359304 | tf_op jit(solution)/shard_map/ppermute | solution.py:434
  151.4 59.4 %collective-permute-start.30 = (bf16[192,2048]{1,0:T(8,128)(2,1)}, bf16[192,2048]{1,0:T(8,128)(2,1)S(1)}, u32[]{:S(2)}, u32[]{:S(2)}) collective-permute-start(bf16[192,2048]{1,0:T(8,128)(2,1)} %collective-permute-done.29.n_own), channel_id=1, source_target_pairs={{0,2},{1,3},{2,0},{3,1},{4,6},{5,7},{6,4},{7,5},{8,10},{9,11},{10,... | collective-permute-start | bytes 2359304 | tf_op jit(solution)/shard_map/ppermute | solution.py:434
  183.4 39.8 %collective-permute-start.27 = (bf16[192,2048]{1,0:T(8,128)(2,1)S(1)}, bf16[192,2048]{1,0:T(8,128)(2,1)S(1)}, u32[]{:S(2)}, u32[]{:S(2)}) collective-permute-start(bf16[192,2048]{1,0:T(8,128)(2,1)S(1)} %copy-done.15), channel_id=1, source_target_pairs={{0,1},{1,0},{2,3},{3,2},{4,5},{5,4},{6,7},{7,6},{8,9},{9,8},{10,11... | collective-permute-start | bytes 2359304 | tf_op jit(solution)/shard_map/ppermute | solution.py:431
  184.6 40.1 %collective-permute-start.48 = (bf16[192,2048]{1,0:T(8,128)(2,1)}, bf16[192,2048]{1,0:T(8,128)(2,1)S(1)}, u32[]{:S(2)}, u32[]{:S(2)}) collective-permute-start(bf16[192,2048]{1,0:T(8,128)(2,1)} %collective-permute-done.29.n_own), channel_id=1, source_target_pairs={{0,12},{1,13},{2,14},{3,15},{4,0},{5,1},{6,2},{7,3},{8,4},{9,5},{1... | collective-permute-start | bytes 2359304 | tf_op jit(solution)/shard_map/ppermute | solution.py:437
  223.2 31.0 %collective-permute-start.37 = (bf16[192,2048]{1,0:T(8,128)(2,1)S(1)}, bf16[192,2048]{1,0:T(8,128)(2,1)S(1)}, u32[]{:S(2)}, u32[]{:S(2)}) collective-permute-start(bf16[192,2048]{1,0:T(8,128)(2,1)S(1)} %collective-permute-done.36.g_own), channel_id=1, source_target_pairs={{0,2},{1,3},{2,0},{3,1},{4,6},{5,7},{6,4},{7,5},{8,10},{9,11},{10,... | collective-permute-start | bytes 2359304 | tf_op jit(solution)/shard_map/ppermute | solution.py:434
  224.8 81.2 %collective-permute-start.41 = (bf16[192,2048]{1,0:T(8,128)(2,1)S(1)}, bf16[192,2048]{1,0:T(8,128)(2,1)S(1)}, u32[]{:S(2)}, u32[]{:S(2)}) collective-permute-start(bf16[192,2048]{1,0:T(8,128)(2,1)S(1)} %collective-permute-done.40.n_own), channel_id=1, source_target_pairs={{0,2},{1,3},{2,0},{3,1},{4,6},{5,7},{6,4},{7,5},{8,10},{9,11},{10,... | collective-permute-start | bytes 2359304 | tf_op jit(solution)/shard_map/ppermute | solution.py:434
  225.3 81.2 %collective-permute-start.46 = (bf16[192,2048]{1,0:T(8,128)(2,1)S(1)}, bf16[192,2048]{1,0:T(8,128)(2,1)S(1)}, u32[]{:S(2)}, u32[]{:S(2)}) collective-permute-start(bf16[192,2048]{1,0:T(8,128)(2,1)S(1)} %collective-permute-done.44.g_own), channel_id=1, source_target_pairs={{0,1},{1,0},{2,3},{3,2},{4,5},{5,4},{6,7},{7,6},{8,9},{9,8},{10,11... | collective-permute-start | bytes 2359304 | tf_op jit(solution)/shard_map/ppermute | solution.py:431
  225.3 52.1 %collective-permute-start.45 = (bf16[192,2048]{1,0:T(8,128)(2,1)S(1)}, bf16[192,2048]{1,0:T(8,128)(2,1)S(1)}, u32[]{:S(2)}, u32[]{:S(2)}) collective-permute-start(bf16[192,2048]{1,0:T(8,128)(2,1)S(1)} %collective-permute-done.44.g_own), channel_id=1, source_target_pairs={{0,2},{1,3},{2,0},{3,1},{4,6},{5,7},{6,4},{7,5},{8,10},{9,11},{10,... | collective-permute-start | bytes 2359304 | tf_op jit(solution)/shard_map/ppermute | solution.py:434
  226.9 66.8 %collective-permute-start.49 = (bf16[192,2048]{1,0:T(8,128)(2,1)S(1)}, bf16[192,2048]{1,0:T(8,128)(2,1)S(1)}, u32[]{:S(2)}, u32[]{:S(2)}) collective-permute-start(bf16[192,2048]{1,0:T(8,128)(2,1)S(1)} %collective-permute-done.48.n_own), channel_id=1, source_target_pairs={{0,2},{1,3},{2,0},{3,1},{4,6},{5,7},{6,4},{7,5},{8,10},{9,11},{10,... | collective-permute-start | bytes 2359304 | tf_op jit(solution)/shard_map/ppermute | solution.py:434
  254.3 52.3 %collective-permute-start.50 = (bf16[192,2048]{1,0:T(8,128)(2,1)S(1)}, bf16[192,2048]{1,0:T(8,128)(2,1)S(1)}, u32[]{:S(2)}, u32[]{:S(2)}) collective-permute-start(bf16[192,2048]{1,0:T(8,128)(2,1)S(1)} %collective-permute-done.48.n_own), channel_id=1, source_target_pairs={{0,1},{1,0},{2,3},{3,2},{4,5},{5,4},{6,7},{7,6},{8,9},{9,8},{10,11... | collective-permute-start | bytes 2359304 | tf_op jit(solution)/shard_map/ppermute | solution.py:431
  277.4 29.6 %collective-permute-start.47 = (bf16[192,2048]{1,0:T(8,128)(2,1)S(1)}, bf16[192,2048]{1,0:T(8,128)(2,1)S(1)}, u32[]{:S(2)}, u32[]{:S(2)}) collective-permute-start(bf16[192,2048]{1,0:T(8,128)(2,1)S(1)} %collective-permute-done.45.g_y), channel_id=1, source_target_pairs={{0,1},{1,0},{2,3},{3,2},{4,5},{5,4},{6,7},{7,6},{8,9},{9,8},{10,11... | collective-permute-start | bytes 2359304 | tf_op jit(solution)/shard_map/ppermute | solution.py:431
  306.0 40.8 %collective-permute-start.38 = (bf16[192,2048]{1,0:T(8,128)(2,1)S(1)}, bf16[192,2048]{1,0:T(8,128)(2,1)S(1)}, u32[]{:S(2)}, u32[]{:S(2)}) collective-permute-start(bf16[192,2048]{1,0:T(8,128)(2,1)S(1)} %collective-permute-done.36.g_own), channel_id=1, source_target_pairs={{0,1},{1,0},{2,3},{3,2},{4,5},{5,4},{6,7},{7,6},{8,9},{9,8},{10,11... | collective-permute-start | bytes 2359304 | tf_op jit(solution)/shard_map/ppermute | solution.py:431
  306.5 40.4 %collective-permute-start.42 = (bf16[192,2048]{1,0:T(8,128)(2,1)S(1)}, bf16[192,2048]{1,0:T(8,128)(2,1)S(1)}, u32[]{:S(2)}, u32[]{:S(2)}) collective-permute-start(bf16[192,2048]{1,0:T(8,128)(2,1)S(1)} %collective-permute-done.40.n_own), channel_id=1, source_target_pairs={{0,1},{1,0},{2,3},{3,2},{4,5},{5,4},{6,7},{7,6},{8,9},{9,8},{10,11... | collective-permute-start | bytes 2359304 | tf_op jit(solution)/shard_map/ppermute | solution.py:431
  306.5 40.3 %collective-permute-start.39 = (bf16[192,2048]{1,0:T(8,128)(2,1)S(1)}, bf16[192,2048]{1,0:T(8,128)(2,1)S(1)}, u32[]{:S(2)}, u32[]{:S(2)}) collective-permute-start(bf16[192,2048]{1,0:T(8,128)(2,1)S(1)} %collective-permute-done.37.g_y), channel_id=1, source_target_pairs={{0,1},{1,0},{2,3},{3,2},{4,5},{5,4},{6,7},{7,6},{8,9},{9,8},{10,11... | collective-permute-start | bytes 2359304 | tf_op jit(solution)/shard_map/ppermute | solution.py:431
  307.0 39.8 %collective-permute-start.43 = (bf16[192,2048]{1,0:T(8,128)(2,1)S(1)}, bf16[192,2048]{1,0:T(8,128)(2,1)S(1)}, u32[]{:S(2)}, u32[]{:S(2)}) collective-permute-start(bf16[192,2048]{1,0:T(8,128)(2,1)S(1)} %collective-permute-done.41.n_y), channel_id=1, source_target_pairs={{0,1},{1,0},{2,3},{3,2},{4,5},{5,4},{6,7},{7,6},{8,9},{9,8},{10,11... | collective-permute-start | bytes 2359304 | tf_op jit(solution)/shard_map/ppermute | solution.py:431
  307.1 110.7 %collective-permute-start.23 = (bf16[2,384,2048]{2,1,0:T(8,128)(2,1)}, bf16[2,384,2048]{2,1,0:T(8,128)(2,1)}, u32[]{:S(2)}, u32[]{:S(2)}) collective-permute-start(bf16[2,384,2048]{2,1,0:T(8,128)(2,1)} %get-tuple-element.104), channel_id=1, source_target_pairs={{0,1},{1,0},{2,3},{3,2},{4,5},{5,4},{6,7},{7,6},{8,9},{9,8},{10,11... | collective-permute-start | bytes 9437192 | tf_op jit(solution)/shard_map/ppermute | solution.py:431
  346.7 74.0 %collective-permute-start.33 = (bf16[2,384,2048]{2,1,0:T(8,128)(2,1)}, bf16[2,384,2048]{2,1,0:T(8,128)(2,1)}, u32[]{:S(2)}, u32[]{:S(2)}) collective-permute-start(bf16[2,384,2048]{2,1,0:T(8,128)(2,1)} %get-tuple-element.118), channel_id=1, source_target_pairs={{0,1},{1,0},{2,3},{3,2},{4,5},{5,4},{6,7},{7,6},{8,9},{9,8},{10,11... | collective-permute-start | bytes 9437192 | tf_op jit(solution)/shard_map/ppermute | solution.py:431
  392.1 60.1 %collective-permute-start.78 = (bf16[640,2048]{1,0:T(8,128)(2,1)}, bf16[640,2048]{1,0:T(8,128)(2,1)}, u32[]{:S(2)}, u32[]{:S(2)}) collective-permute-start(bf16[640,2048]{1,0:T(8,128)(2,1)} %add_convert_fusion), channel_id=1, source_target_pairs={{0,16},{16,0},{1,17},{17,1},{2,18},{18,2},{3,19},{19,3},{4,20},{20... | collective-permute-start | bytes 7864328 | tf_op jit(solution)/shard_map/ppermute | solution.py:447
  393.6 61.5 %collective-permute-start.54 = (bf16[2,384,2048]{2,1,0:T(8,128)(2,1)}, bf16[2,384,2048]{2,1,0:T(8,128)(2,1)}, u32[]{:S(2)}, u32[]{:S(2)}) collective-permute-start(bf16[2,384,2048]{2,1,0:T(8,128)(2,1)} %get-tuple-element.146), channel_id=1, source_target_pairs={{0,1},{1,0},{2,3},{3,2},{4,5},{5,4},{6,7},{7,6},{8,9},{9,8},{10,11... | collective-permute-start | bytes 9437192 | tf_op jit(solution)/shard_map/ppermute | solution.py:431
  408.3 122.0 %collective-permute-start.58 = (f32[16,64,896]{2,1,0:T(8,128)}, f32[16,64,896]{2,1,0:T(8,128)}, u32[]{:S(2)}, u32[]{:S(2)}) collective-permute-start(f32[16,64,896]{2,1,0:T(8,128)} %get-tuple-element.152), channel_id=1, source_target_pairs={{0,16},{16,0},{1,17},{17,1},{2,18},{18,2},{3,19},{19,3},{4,20},{20... | collective-permute-start | bytes 11010056 | tf_op jit(solution)/shard_map/ppermute | solution.py:447
  417.8 134.5 %collective-permute-start.52 = (bf16[2,384,2048]{2,1,0:T(8,128)(2,1)}, bf16[2,384,2048]{2,1,0:T(8,128)(2,1)}, u32[]{:S(2)}, u32[]{:S(2)}) collective-permute-start(bf16[2,384,2048]{2,1,0:T(8,128)(2,1)} %get-tuple-element.144), channel_id=1, source_target_pairs={{0,1},{1,0},{2,3},{3,2},{4,5},{5,4},{6,7},{7,6},{8,9},{9,8},{10,11... | collective-permute-start | bytes 9437192 | tf_op jit(solution)/shard_map/ppermute | solution.py:431
  425.0 206.1 %collective-permute-start.34 = (bf16[2,192,2048]{2,1,0:T(8,128)(2,1)}, bf16[2,192,2048]{2,1,0:T(8,128)(2,1)}, u32[]{:S(2)}, u32[]{:S(2)}) collective-permute-start(bf16[2,192,2048]{2,1,0:T(8,128)(2,1)} %add_convert_fusion.6), channel_id=1, source_target_pairs={{0,2},{1,3},{2,0},{3,1},{4,6},{5,7},{6,4},{7,5},{8,10},{9,11},{10,... | collective-permute-start | bytes 4718600 | tf_op jit(solution)/shard_map/ppermute | solution.py:434
  458.6 99.0 %collective-permute-start.55 = (bf16[2,192,2048]{2,1,0:T(8,128)(2,1)}, bf16[2,192,2048]{2,1,0:T(8,128)(2,1)}, u32[]{:S(2)}, u32[]{:S(2)}) collective-permute-start(bf16[2,192,2048]{2,1,0:T(8,128)(2,1)} %add_convert_fusion.3), channel_id=1, source_target_pairs={{0,2},{1,3},{2,0},{3,1},{4,6},{5,7},{6,4},{7,5},{8,10},{9,11},{10,... | collective-permute-start | bytes 4718600 | tf_op jit(solution)/shard_map/ppermute | solution.py:434
  557.6 80.2 %collective-permute-start.53 = (bf16[2,192,2048]{2,1,0:T(8,128)(2,1)S(1)}, bf16[2,192,2048]{2,1,0:T(8,128)(2,1)S(1)}, u32[]{:S(2)}, u32[]{:S(2)}) collective-permute-start(bf16[2,192,2048]{2,1,0:T(8,128)(2,1)S(1)} %add_convert_fusion.4), channel_id=1, source_target_pairs={{0,2},{1,3},{2,0},{3,1},{4,6},{5,7},{6,4},{7,5},{8,10},{9,11},{10,... | collective-permute-start | bytes 4718600 | tf_op jit(solution)/shard_map/ppermute | solution.py:434
  563.2 74.7 %collective-permute-start.56 = (bf16[2,192,2048]{2,1,0:T(8,128)(2,1)S(1)}, bf16[2,192,2048]{2,1,0:T(8,128)(2,1)S(1)}, u32[]{:S(2)}, u32[]{:S(2)}) collective-permute-start(bf16[2,192,2048]{2,1,0:T(8,128)(2,1)S(1)} %add_convert_fusion.2), channel_id=1, source_target_pairs={{0,12},{1,13},{2,14},{3,15},{4,0},{5,1},{6,2},{7,3},{8,4},{9,5},{1... | collective-permute-start | bytes 4718600 | tf_op jit(solution)/shard_map/ppermute | solution.py:437
  568.5 72.3 %collective-permute-start.24 = (bf16[2,192,2048]{2,1,0:T(8,128)(2,1)S(1)}, bf16[2,192,2048]{2,1,0:T(8,128)(2,1)S(1)}, u32[]{:S(2)}, u32[]{:S(2)}) collective-permute-start(bf16[2,192,2048]{2,1,0:T(8,128)(2,1)S(1)} %add_convert_fusion.7), channel_id=1, source_target_pairs={{0,2},{1,3},{2,0},{3,1},{4,6},{5,7},{6,4},{7,5},{8,10},{9,11},{10,... | collective-permute-start | bytes 4718600 | tf_op jit(solution)/shard_map/ppermute | solution.py:434
  576.9 54.1 %collective-permute-start.75 = (bf16[2,64,896]{2,1,0:T(8,128)(2,1)S(1)}, bf16[2,64,896]{2,1,0:T(8,128)(2,1)S(1)}, u32[]{:S(2)}, u32[]{:S(2)}) collective-permute-start(bf16[2,64,896]{2,1,0:T(8,128)(2,1)S(1)} %get-tuple-element.231), channel_id=1, source_target_pairs={{0,2},{1,3},{2,0},{3,1},{4,6},{5,7},{6,4},{7,5},{8,10},{9,11},{10,... | collective-permute-start | bytes 688136 | tf_op jit(solution)/shard_map/ppermute | solution.py:434
  637.9 108.0 %collective-permute-start.35 = (bf16[2,192,2048]{2,1,0:T(8,128)(2,1)S(1)}, bf16[2,192,2048]{2,1,0:T(8,128)(2,1)S(1)}, u32[]{:S(2)}, u32[]{:S(2)}) collective-permute-start(bf16[2,192,2048]{2,1,0:T(8,128)(2,1)S(1)} %add_convert_fusion.5), channel_id=1, source_target_pairs={{0,4},{1,5},{2,6},{3,7},{4,8},{5,9},{6,10},{7,11},{8,12},{9,13},{1... | collective-permute-start | bytes 4718600 | tf_op jit(solution)/shard_map/ppermute | solution.py:437
  640.9 106.0 %collective-permute-start.57 = (bf16[2,192,2048]{2,1,0:T(8,128)(2,1)S(1)}, bf16[2,192,2048]{2,1,0:T(8,128)(2,1)S(1)}, u32[]{:S(2)}, u32[]{:S(2)}) collective-permute-start(bf16[2,192,2048]{2,1,0:T(8,128)(2,1)S(1)} %add_convert_fusion.1), channel_id=1, source_target_pairs={{0,12},{1,13},{2,14},{3,15},{4,0},{5,1},{6,2},{7,3},{8,4},{9,5},{1... | collective-permute-start | bytes 4718600 | tf_op jit(solution)/shard_map/ppermute | solution.py:437
  646.8 89.7 %collective-permute-start.60 = (bf16[4,64,896]{2,1,0:T(8,128)(2,1)S(1)}, bf16[4,64,896]{2,1,0:T(8,128)(2,1)S(1)}, u32[]{:S(2)}, u32[]{:S(2)}) collective-permute-start(bf16[4,64,896]{2,1,0:T(8,128)(2,1)S(1)} %add_convert_fusion.11), channel_id=1, source_target_pairs={{0,8},{1,9},{2,10},{3,11},{4,12},{5,13},{6,14},{7,15},{8,0},{9,1},... | collective-permute-start | bytes 1376264 | tf_op jit(solution)/shard_map/ppermute | solution.py:437
  647.0 137.4 %collective-permute-start.77 = (bf16[4,64,896]{2,1,0:T(8,128)(2,1)S(1)}, bf16[4,64,896]{2,1,0:T(8,128)(2,1)S(1)}, u32[]{:S(2)}, u32[]{:S(2)}) collective-permute-start(bf16[4,64,896]{2,1,0:T(8,128)(2,1)S(1)} %bitcast.163), channel_id=1, source_target_pairs={{0,16},{16,0},{1,17},{17,1},{2,18},{18,2},{3,19},{19,3},{4,20},{20... | collective-permute-start | bytes 1376264 | tf_op jit(solution)/shard_map/ppermute | solution.py:447
  656.1 82.0 %collective-permute-start.71 = (bf16[2,64,896]{2,1,0:T(8,128)(2,1)S(1)}, bf16[2,64,896]{2,1,0:T(8,128)(2,1)S(1)}, u32[]{:S(2)}, u32[]{:S(2)}) collective-permute-start(bf16[2,64,896]{2,1,0:T(8,128)(2,1)S(1)} %get-tuple-element.227), channel_id=1, source_target_pairs={{0,2},{1,3},{2,0},{3,1},{4,6},{5,7},{6,4},{7,5},{8,10},{9,11},{10,... | collective-permute-start | bytes 688136 | tf_op jit(solution)/shard_map/ppermute | solution.py:434
  751.8 32.5 %collective-permute-start.73 = (bf16[4,64,896]{2,1,0:T(8,128)(2,1)S(1)}, bf16[4,64,896]{2,1,0:T(8,128)(2,1)S(1)}, u32[]{:S(2)}, u32[]{:S(2)}) collective-permute-start(bf16[4,64,896]{2,1,0:T(8,128)(2,1)S(1)} %bitcast.165), channel_id=1, source_target_pairs={{0,16},{16,0},{1,17},{17,1},{2,18},{18,2},{3,19},{19,3},{4,20},{20... | collective-permute-start | bytes 1376264 | tf_op jit(solution)/shard_map/ppermute | solution.py:447
  755.1 29.3 %collective-permute-start.68 = (bf16[4,64,896]{2,1,0:T(8,128)(2,1)S(1)}, bf16[4,64,896]{2,1,0:T(8,128)(2,1)S(1)}, u32[]{:S(2)}, u32[]{:S(2)}) collective-permute-start(bf16[4,64,896]{2,1,0:T(8,128)(2,1)S(1)} %bitcast.167), channel_id=1, source_target_pairs={{0,16},{16,0},{1,17},{17,1},{2,18},{18,2},{3,19},{19,3},{4,20},{20... | collective-permute-start | bytes 1376264 | tf_op jit(solution)/shard_map/ppermute | solution.py:447
  (96 other events, 1277.6 us)
where the time goes:
time: 810 us; the launch traced here: 802 us
  waiting for transfers between devices  365 us (45%)
  Pallas kernels  181 us (22%)
  starting transfers between devices  102 us (13%)
  other arithmetic  83.3 us (10%)
  matrix products  50.5 us (6%)
  local copies, waits for them, and re-layouts  18.1 us (2%)
    ppermute x21, waiting for transfers between devices, along_z(): return lax.ppermute(x, 'shard', up_z[n % NZ])  124 us
    ppermute x15, waiting for transfers between devices, next_copy(): lax.ppermute(x, 'replica', [(i, (i + n) % copies) for i in range(copies)])  121 us
    ppermute x22, waiting for transfers between devices, across_y(): return lax.ppermute(x, 'shard', swap_y)  119 us
    pallas_call x4, Pallas kernels, run_chunk(): pl.pallas_call(chunk_kernel, in_specs=[anywhere] * 8 + [here] * 8, out_sp...  109 us
    ppermute x21, starting transfers between devices, along_z(): return lax.ppermute(x, 'shard', up_z[n % NZ])  53.6 us
    dot_general x8, matrix products, dot(): return lax.dot_general(a, b, dims, preferred_element_type=F32)  50.5 us
    pallas_call x5, Pallas kernels, split_sum(): pl.pallas_call(kernel, grid_spec=pltpu.PrefetchScalarGridSpec(num_scalar_...  34 us
    ppermute x22, starting transfers between devices, across_y(): return lax.ppermute(x, 'shard', swap_y)  27.9 us
  transfers between devices with their start and end apart: 85, of which 27 were waited for; matrix products, arithmetic and copies ran while one was open for 18% of the time, Pallas kernels for 23%

commit v1 on v0

--- a/solution.py
+++ b/solution.py
@@ -38,8 +38,8 @@
 def adamw(weight, grad, first, second, decay):
     first = BETA_ONE * first + (1.0 - BETA_ONE) * grad
     second = BETA_TWO * second + (1.0 - BETA_TWO) * grad * grad
-    first_hat = first / (1.0 - BETA_ONE**ADAM_STEP)
-    second_hat = second / (1.0 - BETA_TWO**ADAM_STEP)
+    first_hat = first * (1.0 / (1.0 - BETA_ONE**ADAM_STEP))
+    second_hat = second * (1.0 / (1.0 - BETA_TWO**ADAM_STEP))
     weight = weight - LEARN_RATE * (first_hat / (jnp.sqrt(second_hat) + ADAM_EPS) + decay * weight)
     return (weight, first, second)
 
@@ -83,7 +83,7 @@
         scores = jnp.where(allowed, dot(qh, k, BY_LAST) * SCORE_SCALE, -1e30)
         peak = jnp.max(scores, axis=1, keepdims=True)
         grown = jnp.exp(scores - peak)
-        probs = grown / jnp.sum(grown, axis=1, keepdims=True)
+        probs = grown * (1.0 / jnp.sum(grown, axis=1, keepdims=True))
         low = probs.astype(LOW)
         attended = attended + dot(low, vh)
         dp = dot(gah, v, BY_LAST)
@@ -306,45 +306,44 @@
     )(place, *pieces)
 
 
-def split_sum(grads, held, place, part, first, blocks, kind):
+def split_sum(grads, held, place, part, first, groups, kind):
+    step = part // 2
+
     def kernel(place_ref, *refs):
-        total = refs[0][...]
-        for ref in refs[1 : len(grads)]:
-            total = total + ref[...]
-        copy = place_ref[RANKS]
-
-        def give(sent, kept):
-            refs[-2][...] = sent.astype(kind)
+        copy = place_ref[NZ + 4]
+        for k in range(4):
+            at = place_ref[NZ + k]
+
+            def total(half):
+                value = refs[0][at, half]
+                for ref in refs[1 : len(grads)]:
+                    value = value + ref[at, half]
+                return value
+
+            refs[-2][k] = total(1 - copy).astype(kind)
+            kept = total(copy)
             for ref in refs[len(grads) : -2]:
-                kept = kept + ref[...]
-            refs[-1][...] = kept
-
-        @pl.when(copy == 0)
-        def _():
-            give(total[:, 1], total[:, 0])
-
-        @pl.when(copy != 0)
-        def _():
-            give(total[:, 0], total[:, 1])
-
-    own = pl.BlockSpec((1, 2, part, PROJ), lambda i, at: (at[first + i], 0, 0, 0))
-    old = pl.BlockSpec((1, part, PROJ), lambda i, at: (first + i, 0, 0))
-    half = pl.BlockSpec((1, part, PROJ), lambda i, at: (i, 0, 0))
+                kept = kept + ref[k]
+            refs[-1][k] = kept
+
+    own = pl.BlockSpec((4, 2, step, PROJ), lambda i, j, at: (at[first + i], 0, j, 0))
+    old = pl.BlockSpec((4, step, PROJ), lambda i, j, at: (first + i, j, 0))
+    half = pl.BlockSpec((4, step, PROJ), lambda i, j, at: (i, j, 0))
     return pl.pallas_call(
         kernel,
         grid_spec=pltpu.PrefetchScalarGridSpec(
             num_scalar_prefetch=1,
-            grid=(blocks,),
+            grid=(groups, 2),
             in_specs=[own] * len(grads) + [old] * len(held),
             out_specs=[half, half],
         ),
         out_shape=[
-            jax.ShapeDtypeStruct((blocks, part, PROJ), kind),
-            jax.ShapeDtypeStruct((blocks, part, PROJ), F32),
+            jax.ShapeDtypeStruct((4 * groups, part, PROJ), kind),
+            jax.ShapeDtypeStruct((4 * groups, part, PROJ), F32),
         ],
         cost_estimate=pl.CostEstimate(
-            flops=8 * blocks * part * PROJ,
-            bytes_accessed=30 * blocks * part * PROJ,
+            flops=32 * groups * part * PROJ,
+            bytes_accessed=120 * groups * part * PROJ,
             transcendentals=0,
         ),
         name="split_sum",
@@ -541,10 +540,11 @@
         part = D // RANKS // 2
         place = table(
             me,
-            lambda z, y, c: [near(z, y, c, n, i, j) for n in GRAD_ORDER for i in (0, 1) for j in (0, 1)],
+            lambda z, y, c: [(z + n) % NZ for n in GRAD_ORDER]
+            + [near(0, y, c, 0, i, j) for i in (0, 1) for j in (0, 1)],
         )
         place = jnp.concatenate([place, copy.reshape(1)])
-        sent, kept = split_sum(grad_in, (), place, part, 0, RANKS, F32)
+        sent, kept = split_sum(grad_in, (), place, part, 0, NZ, F32)
         return place, kept, next_copy(sent, 1)
 
     def finish_in(grad_in, early, w_in, m_in, v_in, me, z, y, c, f, copy):
@@ -555,7 +555,7 @@
             halves = []
             for i, n in enumerate(GRAD_ORDER):
                 sent, base = split_sum(
-                    grad_in[EARLY:], (kept, heard), place, part, 4 * i, 4, LOW
+                    grad_in[EARLY:], (kept, heard), place, part, i, 1, LOW
                 )
                 late = next_copy(sent, 1)
                 block = (base + late).astype(LOW)
@@ -672,10 +672,10 @@
             over = across_y(sent)
             own = near[:, :length] + came[:, :length].astype(F32) + over.astype(F32)
             if carried is not None:
-                own = own + carried
+                own = own + carried.astype(F32)
             if n == 0:
                 return own
-            return along_z(own.astype(LOW), 1 if n == 3 else 3).astype(F32)
+            return along_z(own.astype(LOW), 1 if n == 3 else 3)
 
         totals = []
         early = None
@@ -686,12 +686,10 @@
             gc = g_chunks[n]
             nc = n_chunks[n]
             if grad_in:
-                gc, nc, last_in, last_pair = lax.optimization_barrier(
-                    (gc, nc, grad_in[-1], grad_pair[-1])
-                )
-                grad_in[-1] = last_in
-                grad_pair[-1] = last_pair
+                gc, nc, grad_in[-1] = lax.optimization_barrier((gc, nc, grad_in[-1]))
             angles = places[n].reshape(4 * length, 1) * freqs
+            cosine = jnp.cos(angles)
+            sine = jnp.sin(angles)
             n_cat, g_cat, ah, gp, far, near, sums = run_chunk(
                 nc,
                 gc,
@@ -699,8 +697,8 @@
                 w_pair,
                 bias_in,
                 bias_tail.reshape(1, D),
-                jnp.cos(angles),
-                jnp.sin(angles),
+                cosine,
+                sine,
                 segs[n].reshape(4 * length, 1),
                 segs[n].reshape(4, 1, length),
             )
@@ -711,8 +709,8 @@
             totals.append(carried)
             if len(grad_in) == EARLY and fold == 1 and copies == 2:
                 early = start_in(grad_in, me, copy)
-        gn_total = sum([part[0] for part in totals[1:]], totals[0][0])
-        out_total = sum([part[1] for part in totals[1:]], totals[0][1])
+        gn_total = sum([part[0].astype(F32) for part in totals[1:]], totals[0][0])
+        out_total = sum([part[1].astype(F32) for part in totals[1:]], totals[0][1])
         proj_sum = sum(proj_sum[1:], proj_sum[0])
         grad_pair = sum(grad_pair[1:], grad_pair[0])
 

time: 810 us -> 833 us (1.028)
  waiting for transfers between devices: 365 us -> 430 us
  starting transfers between devices: 102 us -> 63.4 us
    ppermute x21, waiting for transfers between devices: 124 us -> 161 us  [along_z(): return lax.ppermute(x, 'shard', up_z[n % NZ])]
    ppermute x21, starting transfers between devices: 53.6 us -> 23.4 us  [along_z(): return lax.ppermute(x, 'shard', up_z[n % NZ])]
    ppermute x22, waiting for transfers between devices: 119 us -> 133 us  [across_y(): return lax.ppermute(x, 'shard', swap_y)]
    ppermute x15, waiting for transfers between devices: 121 us -> 134 us  [next_copy(): lax.ppermute(x, 'replica', [(i, (i + n) % copies) for i in range(copies)])]
    convert_element_type x6 -> x3, other arithmetic: 20.7 us -> 9.1 us  [scatter_add(): return along_z(own.astype(LOW), 1 if n == 3 else 3)]
    ppermute x22, starting transfers between devices: 27.9 us -> 19.4 us  [across_y(): return lax.ppermute(x, 'shard', swap_y)]
  transfers between devices with their start and end apart: 85 -> 85, of which waited for: 27 -> 26; matrix products, arithmetic and copies ran while one was open for 18% -> 17% of each run, Pallas kernels for 23% -> 21%
where the time goes in v1:
time: 833 us; the launch traced here: 825 us
  waiting for transfers between devices  430 us (52%)
  Pallas kernels  176 us (21%)
  other arithmetic  81.4 us (10%)
  starting transfers between devices  63.4 us (8%)
  matrix products  47.5 us (6%)
  local copies, waits for them, and re-layouts  24.1 us (3%)
    ppermute x21, waiting for transfers between devices, along_z(): return lax.ppermute(x, 'shard', up_z[n % NZ])  161 us
    ppermute x15, waiting for transfers between devices, next_copy(): lax.ppermute(x, 'replica', [(i, (i + n) % copies) for i in range(copies)])  134 us
    ppermute x22, waiting for transfers between devices, across_y(): return lax.ppermute(x, 'shard', swap_y)  133 us
    pallas_call x4, Pallas kernels, run_chunk(): pl.pallas_call(chunk_kernel, in_specs=[anywhere] * 8 + [here] * 8, out_sp...  111 us
    dot_general x8, matrix products, dot(): return lax.dot_general(a, b, dims, preferred_element_type=F32)  47.5 us
    pallas_call x5, Pallas kernels, split_sum(): pl.pallas_call(kernel, grid_spec=pltpu.PrefetchScalarGridSpec(num_scalar_...  27.8 us
    pallas_call x2, Pallas kernels, adamw_rows(): pl.pallas_call(kernel, grid_spec=pltpu.PrefetchScalarGridSpec(num_scalar_...  27.5 us
    ppermute x21, starting transfers between devices, along_z(): return lax.ppermute(x, 'shard', up_z[n % NZ])  23.4 us
  transfers between devices with their start and end apart: 85, of which 26 were waited for; matrix products, arithmetic and copies ran while one was open for 17% of the time, Pallas kernels for 21%

profile of v1, /device:TPU:0, one launch (start us, length us, event | category | flops | bytes accessed | tf_op | source)
XLA Modules:
  0.0 824.6 jit_solution(12764063960974549711)
XLA Ops:
  3.6 5.1 collective-permute-start.2
  17.2 4.9 ranks_first.1
  24.6 17.8 %collective-permute-done.3 = f32[4,640]{1,0:T(4,128)S(1)} collective-permute-done((f32[4,640]{1,0:T(4,128)S(1)}, f32[4,640]{1,0:T(4,128)S(1)}, u32[]{:S(2)}, u32[]{:S(2)}) %collective-permute-start.3) | collective-permute-done | bytes 10272 | tf_op jit(solution)/shard_map/ppermute | solution.py:433
  49.0 30.4 %collective-permute-done.13 = bf16[2,2,64,896]{3,2,0,1:T(8,128)(2,1)S(1)} collective-permute-done((bf16[2,2,64,896]{3,2,0,1:T(8,128)(2,1)S(1)}, bf16[2,2,64,896]{3,2,0,1:T(8,128)(2,1)S(1)}, u32[]{:S(2)}, u32[]{:S(2)}) %collective-permute-start.13) | collective-permute-done | bytes 458784 | tf_op jit(solution)/shard_map/ppermute | solution.py:436
  84.9 3.6 collective-permute-done.12
  89.6 36.9 %collective-permute-done.17 = bf16[2,2,64,896]{3,2,1,0:T(8,128)(2,1)S(1)} collective-permute-done((bf16[2,2,64,896]{3,2,1,0:T(8,128)(2,1)S(1)}, bf16[2,2,64,896]{3,2,1,0:T(8,128)(2,1)S(1)}, u32[]{:S(2)}, u32[]{:S(2)}) %collective-permute-start.17) | collective-permute-done | bytes 458784 | tf_op jit(solution)/shard_map/ppermute | solution.py:436
  128.9 5.6 collective-permute-done.16
  137.8 4.2 collective-permute-done.18
  163.3 9.3 %collective-permute-done.20.refs_5_ = bf16[4,64,896]{2,1,0:T(8,128)(2,1)} collective-permute-done((bf16[4,64,896]{2,1,0:T(8,128)(2,1)}, bf16[4,64,896]{2,1,0:T(8,128)(2,1)}, u32[]{:S(2)}, u32[]{:S(2)}) %collective-permute-start.20) | collective-permute-done | bytes 458784 | tf_op jit(solution)/shard_map/ppermute | solution.py:446
  172.7 9.8 %collective-permute-done.21.refs_6_ = bf16[4,64,896]{2,1,0:T(8,128)(2,1)} collective-permute-done((bf16[4,64,896]{2,1,0:T(8,128)(2,1)}, bf16[4,64,896]{2,1,0:T(8,128)(2,1)}, u32[]{:S(2)}, u32[]{:S(2)}) %collective-permute-start.21) | collective-permute-done | bytes 458784 | tf_op jit(solution)/shard_map/ppermute | solution.py:446
  183.0 6.9 collective-permute-done.22.refs_7_
  196.2 7.8 multiply_sine_fusion
  204.0 4.8 rows_home.1.w_cols
  214.4 28.1 %chunk.4 = (bf16[768,2048]{1,0:T(8,128)(2,1)}, bf16[768,2048]{1,0:T(8,128)(2,1)}, bf16[768,640]{1,0:T(8,128)(2,1)S(1)}, bf16[768,896]{1,0:T(8,128)(2,1)S(1)}, bf...) custom-call(bf16[192,2048]{1,0:T(8,128)(2,1)S(1)} %fusion.8.n_own, ...), custom_call_target="tpu_custom_call" | custom-call | flops 9732489216 | bytes 37748736 | tf_op jit(solution)/shard_map/chunk/pallas_call | solution.py:206
  242.6 7.4 fusion.62
  256.2 28.2 %chunk.5 = (bf16[768,2048]{1,0:T(8,128)(2,1)}, bf16[768,2048]{1,0:T(8,128)(2,1)}, bf16[768,640]{1,0:T(8,128)(2,1)S(1)}, bf16[768,896]{1,0:T(8,128)(2,1)S(1)}, bf...) custom-call(bf16[192,2048]{1,0:T(8,128)(2,1)} %collective-permute-done.29.n_own, ...), custom_call_target="tpu_custom_call" | custom-call | flops 9732489216 | bytes 37748736 | tf_op jit(solution)/shard_map/chunk/pallas_call | solution.py:206
  284.6 19.6 %collective-permute-done.45.g_y = bf16[192,2048]{1,0:T(8,128)(2,1)S(1)} collective-permute-done((bf16[192,2048]{1,0:T(8,128)(2,1)}, bf16[192,2048]{1,0:T(8,128)(2,1)S(1)}, u32[]{:S(2)}, u32[]{:S(2)}) %collective-permute-start.45) | collective-permute-done | bytes 786464 | tf_op jit(solution)/shard_map/ppermute | solution.py:433
  304.2 16.3 %collective-permute-done.49.n_y = bf16[192,2048]{1,0:T(8,128)(2,1)S(1)} collective-permute-done((bf16[192,2048]{1,0:T(8,128)(2,1)S(1)}, bf16[192,2048]{1,0:T(8,128)(2,1)S(1)}, u32[]{:S(2)}, u32[]{:S(2)}) %collective-permute-start.49) | collective-permute-done | bytes 786464 | tf_op jit(solution)/shard_map/ppermute | solution.py:433
  320.5 6.6 fusion.66
  327.1 5.5 fusion.63
  336.2 27.8 %chunk.6 = (bf16[768,2048]{1,0:T(8,128)(2,1)}, bf16[768,2048]{1,0:T(8,128)(2,1)}, bf16[768,640]{1,0:T(8,128)(2,1)S(1)}, bf16[768,896]{1,0:T(8,128)(2,1)S(1)}, bf...) custom-call(bf16[192,2048]{1,0:T(8,128)(2,1)S(1)} %collective-permute-done.48.n_own, ...), custom_call_target="tpu_custom_call" | custom-call | flops 9732489216 | bytes 37748736 | tf_op jit(solution)/shard_map/chunk/pallas_call | solution.py:206
  364.1 7.3 fusion.64
  371.4 27.0 %chunk.7 = (bf16[768,2048]{1,0:T(8,128)(2,1)}, bf16[768,2048]{1,0:T(8,128)(2,1)}, bf16[768,640]{1,0:T(8,128)(2,1)S(1)}, bf16[768,896]{1,0:T(8,128)(2,1)S(1)}, bf...) custom-call(bf16[192,2048]{1,0:T(8,128)(2,1)} %collective-permute-done.40.n_own, ...), custom_call_target="tpu_custom_call" | custom-call | flops 9732489216 | bytes 37748736 | tf_op jit(solution)/shard_map/chunk/pallas_call | solution.py:206
  398.5 4.7 fusion.68
  405.5 6.4 add_convert_fusion
  415.5 10.8 %split_sum.5 = (f32[16,64,896]{2,1,0:T(8,128)}, f32[16,64,896]{2,1,0:T(8,128)}) custom-call(s32[9]{0:T(128)} %pad_add_fusion.3.place_ref, f32[16,2,64,896]{3,2,1,0:T(8,128)} %bitcast.155, f32[16,2,64,896]{3,2,1,0:T(8,128)} %bitcast.156), custom_call_target="tpu_custom_call" | custom-call | flops 7340032 | bytes 27525120 | tf_op jit(solution)/shard_map/split_sum/pallas_call | solution.py:332
  427.2 7.3 fusion.65
  437.4 4.2 add_convert_fusion.6
  442.0 30.0 %collective-permute-done.78 = bf16[640,2048]{1,0:T(8,128)(2,1)} collective-permute-done((bf16[640,2048]{1,0:T(8,128)(2,1)}, bf16[640,2048]{1,0:T(8,128)(2,1)}, u32[]{:S(2)}, u32[]{:S(2)}) %collective-permute-start.78) | collective-permute-done | bytes 2621472 | tf_op jit(solution)/shard_map/ppermute | solution.py:446
  472.0 3.6 convert_add_fusion
  479.3 9.9 %multiply_subtract_fusion = (f32[512,2048]{1,0:T(8,128)}, f32[512,2048]{1,0:T(8,128)}, f32[512,2048]{1,0:T(8,128)}, f32[512,2048]{1,0:T(8,128)}) fusion(f32[512,2048]{1,0:T(8,128)S(1)} %copy-done.26, f32[512,2048]{1,0:T(8,128)} %param.30, f32[512,2048]{1,0:T(8,128)} %param.31, f32[640,2048]{1,0:T(8,128)S(1)} %convert_add_fusion), kind=kLoop, calls=%fused_computation.5 | loop fusion | flops 15728640 | bytes 33554432 | tf_op jit(solution)/shard_map/sub | solution.py:43
  491.5 58.6 %collective-permute-done.58.refs_3_ = f32[16,64,896]{2,1,0:T(8,128)} collective-permute-done((f32[16,64,896]{2,1,0:T(8,128)}, f32[16,64,896]{2,1,0:T(8,128)}, u32[]{:S(2)}, u32[]{:S(2)}) %collective-permute-start.58) | collective-permute-done | bytes 3670048 | tf_op jit(solution)/shard_map/ppermute | solution.py:446
  550.2 4.2 split_sum.9
  555.9 4.2 split_sum.8
  560.6 4.3 split_sum.7
  564.9 4.2 split_sum.6
  576.1 3.7 add_convert_fusion.2
  580.1 7.5 collective-permute-done.64
  588.2 8.0 collective-permute-done.59
  596.7 52.5 %collective-permute-done.75 = bf16[2,64,896]{2,1,0:T(8,128)(2,1)S(1)} collective-permute-done((bf16[2,64,896]{2,1,0:T(8,128)(2,1)S(1)}, bf16[2,64,896]{2,1,0:T(8,128)(2,1)S(1)}, u32[]{:S(2)}, u32[]{:S(2)}) %collective-permute-start.75) | collective-permute-done | bytes 229408 | tf_op jit(solution)/shard_map/ppermute | solution.py:433
  658.8 3.9 collective-permute-start.57
  666.7 34.9 %collective-permute-done.65 = bf16[4,64,896]{2,1,0:T(8,128)(2,1)S(1)} collective-permute-done((bf16[4,64,896]{2,1,0:T(8,128)(2,1)S(1)}, bf16[4,64,896]{2,1,0:T(8,128)(2,1)S(1)}, u32[]{:S(2)}, u32[]{:S(2)}) %collective-permute-start.65) | collective-permute-done | bytes 458784 | tf_op jit(solution)/shard_map/ppermute | solution.py:436
  702.1 55.6 %collective-permute-done.60 = bf16[4,64,896]{2,1,0:T(8,128)(2,1)S(1)} collective-permute-done((bf16[4,64,896]{2,1,0:T(8,128)(2,1)S(1)}, bf16[4,64,896]{2,1,0:T(8,128)(2,1)S(1)}, u32[]{:S(2)}, u32[]{:S(2)}) %collective-permute-start.60) | collective-permute-done | bytes 458784 | tf_op jit(solution)/shard_map/ppermute | solution.py:436
  759.9 6.3 collective-permute-done.66
  766.2 3.6 collective-permute-done.61
  780.1 3.7 collective-permute-done.83
  788.2 13.7 %adamw_rows.2 = (f32[128,14336]{1,0:T(8,128)}, f32[128,14336]{1,0:T(8,128)}, f32[128,14336]{1,0:T(8,128)}, f32[128,14336]{1,0:T(8,128)}) custom-call(s32[17]{0:T(128)} %get-tuple-element.265.slots_ref, f32[128,14336]{1,0:T(8,128)} %w_ref.5, f32[128,14336]{1,0:T(8,128)} %m_ref.3, f32[128,14336]{1,0:T(8,128)} %v_ref.3, ...), custom_call_target="tpu_custom_call" | custom-call | flops 18350080 | bytes 27525120 | tf_op jit(solution)/shard_map/adamw_rows/pallas_call | solution.py:389
  809.6 13.8 %adamw_rows.3 = (f32[128,14336]{1,0:T(8,128)}, f32[128,14336]{1,0:T(8,128)}, f32[128,14336]{1,0:T(8,128)}, f32[128,14336]{1,0:T(8,128)}) custom-call(s32[17]{0:T(128)} %get-tuple-element.266.slots_ref, f32[128,14336]{1,0:T(8,128)} %w_ref.5, f32[128,14336]{1,0:T(8,128)} %m_ref.3, ...), custom_call_target="tpu_custom_call", output_to_operand_aliasing={{0}: (5, {}), {1}: (6, {}), {2}: (7, {}), {3}: (8, {})} | custom-call | flops 18350080 | bytes 27525120 | tf_op jit(solution)/shard_map/adamw_rows/pallas_call | solution.py:389
  (398 shorter events, 141.5 us)
Async XLA Ops:
  9.7 70.4 %collective-permute-start.25 = (bf16[192,2048]{1,0:T(8,128)(2,1)}, bf16[192,2048]{1,0:T(8,128)(2,1)}, u32[]{:S(2)}, u32[]{:S(2)}) collective-permute-start(bf16[192,2048]{1,0:T(8,128)(2,1)} %g_own.1), channel_id=1, source_target_pairs={{0,12},{1,13},{2,14},{3,15},{4,0},{5,1},{6,2},{7,3},{8,4},{9,5},{1... | collective-permute-start | bytes 2359304 | tf_op jit(solution)/shard_map/ppermute | solution.py:436
  12.5 70.4 %collective-permute-start.9 = (bf16[192,2048]{1,0:T(8,128)(2,1)}, bf16[192,2048]{1,0:T(8,128)(2,1)S(1)}, u32[]{:S(2)}, u32[]{:S(2)}) collective-permute-start(bf16[192,2048]{1,0:T(8,128)(2,1)} %g_own.1), channel_id=1, source_target_pairs={{0,1},{1,0},{2,3},{3,2},{4,5},{5,4},{6,7},{7,6},{8,9},{9,8},{10,11... | collective-permute-start | bytes 2359304 | tf_op jit(solution)/shard_map/ppermute | solution.py:430
  22.1 62.7 %collective-permute-start.8 = (bf16[192,2048]{1,0:T(8,128)(2,1)S(1)}, bf16[192,2048]{1,0:T(8,128)(2,1)}, u32[]{:S(2)}, u32[]{:S(2)}) collective-permute-start(bf16[192,2048]{1,0:T(8,128)(2,1)S(1)} %copy-done), channel_id=1, source_target_pairs={{0,2},{1,3},{2,0},{3,1},{4,6},{5,7},{6,4},{7,5},{8,10},{9,11},{10,... | collective-permute-start | bytes 2359304 | tf_op jit(solution)/shard_map/ppermute | solution.py:433
  47.0 32.3 %collective-permute-start.13 = (bf16[2,2,64,896]{3,2,0,1:T(8,128)(2,1)S(1)}, bf16[2,2,64,896]{3,2,0,1:T(8,128)(2,1)S(1)}, u32[]{:S(2)}, u32[]{:S(2)}) collective-permute-start(bf16[2,2,64,896]{3,2,0,1:T(8,128)(2,1)S(1)} %pad_maximum_fusion.4), channel_id=1, source_target_pairs={{0,8},{1,9},{2,10},{3,11},{4,12},{5,13},{6,14},{7,15},{8,0},{9,1},... | collective-permute-start | bytes 1376264 | tf_op jit(solution)/shard_map/ppermute | solution.py:436
  48.7 32.9 %collective-permute-start.15 = (bf16[2,2,64,896]{3,2,0,1:T(8,128)(2,1)S(1)}, bf16[2,2,64,896]{3,2,0,1:T(8,128)(2,1)S(1)}, u32[]{:S(2)}, u32[]{:S(2)}) collective-permute-start(bf16[2,2,64,896]{3,2,0,1:T(8,128)(2,1)S(1)} %pad_maximum_fusion.6), channel_id=1, source_target_pairs={{0,4},{1,5},{2,6},{3,7},{4,8},{5,9},{6,10},{7,11},{8,12},{9,13},{1... | collective-permute-start | bytes 1376264 | tf_op jit(solution)/shard_map/ppermute | solution.py:436
  79.4 47.1 %collective-permute-start.17 = (bf16[2,2,64,896]{3,2,1,0:T(8,128)(2,1)S(1)}, bf16[2,2,64,896]{3,2,1,0:T(8,128)(2,1)S(1)}, u32[]{:S(2)}, u32[]{:S(2)}) collective-permute-start(bf16[2,2,64,896]{3,2,1,0:T(8,128)(2,1)S(1)} %pad_maximum_fusion.8), channel_id=1, source_target_pairs={{0,12},{1,13},{2,14},{3,15},{4,0},{5,1},{6,2},{7,3},{8,4},{9,5},{1... | collective-permute-start | bytes 1376264 | tf_op jit(solution)/shard_map/ppermute | solution.py:436
  81.6 44.8 %collective-permute-start.14 = (bf16[2,64,896]{2,1,0:T(8,128)(2,1)S(1)}, bf16[2,64,896]{2,1,0:T(8,128)(2,1)S(1)}, u32[]{:S(2)}, u32[]{:S(2)}) collective-permute-start(bf16[2,64,896]{2,1,0:T(8,128)(2,1)S(1)} %get-tuple-element.231), channel_id=1, source_target_pairs={{0,2},{1,3},{2,0},{3,1},{4,6},{5,7},{6,4},{7,5},{8,10},{9,11},{10,... | collective-permute-start | bytes 688136 | tf_op jit(solution)/shard_map/ppermute | solution.py:433
  82.9 66.3 %collective-permute-start.36 = (bf16[192,2048]{1,0:T(8,128)(2,1)S(1)}, bf16[192,2048]{1,0:T(8,128)(2,1)S(1)}, u32[]{:S(2)}, u32[]{:S(2)}) collective-permute-start(bf16[192,2048]{1,0:T(8,128)(2,1)S(1)} %copy-done), channel_id=1, source_target_pairs={{0,4},{1,5},{2,6},{3,7},{4,8},{5,9},{6,10},{7,11},{8,12},{9,13},{1... | collective-permute-start | bytes 2359304 | tf_op jit(solution)/shard_map/ppermute | solution.py:436
  84.9 65.7 %collective-permute-start.40 = (bf16[192,2048]{1,0:T(8,128)(2,1)S(1)}, bf16[192,2048]{1,0:T(8,128)(2,1)}, u32[]{:S(2)}, u32[]{:S(2)}) collective-permute-start(bf16[192,2048]{1,0:T(8,128)(2,1)S(1)} %fusion.8.n_own), channel_id=1, source_target_pairs={{0,4},{1,5},{2,6},{3,7},{4,8},{5,9},{6,10},{7,11},{8,12},{9,13},{1... | collective-permute-start | bytes 2359304 | tf_op jit(solution)/shard_map/ppermute | solution.py:436
  88.6 62.6 %collective-permute-start.29 = (bf16[192,2048]{1,0:T(8,128)(2,1)S(1)}, bf16[192,2048]{1,0:T(8,128)(2,1)}, u32[]{:S(2)}, u32[]{:S(2)}) collective-permute-start(bf16[192,2048]{1,0:T(8,128)(2,1)S(1)} %fusion.8.n_own), channel_id=1, source_target_pairs={{0,12},{1,13},{2,14},{3,15},{4,0},{5,1},{6,2},{7,3},{8,4},{9,5},{1... | collective-permute-start | bytes 2359304 | tf_op jit(solution)/shard_map/ppermute | solution.py:436
  151.1 31.3 %collective-permute-start.21 = (bf16[4,64,896]{2,1,0:T(8,128)(2,1)}, bf16[4,64,896]{2,1,0:T(8,128)(2,1)}, u32[]{:S(2)}, u32[]{:S(2)}) collective-permute-start(bf16[4,64,896]{2,1,0:T(8,128)(2,1)} %pad_maximum_fusion.7.refs_2_), channel_id=1, source_target_pairs={{0,16},{16,0},{1,17},{17,1},{2,18},{18,2},{3,19},{19,3},{4,20},{20... | collective-permute-start | bytes 1376264 | tf_op jit(solution)/shard_map/ppermute | solution.py:446
  152.6 37.3 %collective-permute-start.22 = (bf16[4,64,896]{2,1,0:T(8,128)(2,1)}, bf16[4,64,896]{2,1,0:T(8,128)(2,1)}, u32[]{:S(2)}, u32[]{:S(2)}) collective-permute-start(bf16[4,64,896]{2,1,0:T(8,128)(2,1)} %pad_maximum_fusion.9.refs_3_), channel_id=1, source_target_pairs={{0,16},{16,0},{1,17},{17,1},{2,18},{18,2},{3,19},{19,3},{4,20},{20... | collective-permute-start | bytes 1376264 | tf_op jit(solution)/shard_map/ppermute | solution.py:446
  160.4 48.4 %collective-permute-start.44 = (bf16[192,2048]{1,0:T(8,128)(2,1)}, bf16[192,2048]{1,0:T(8,128)(2,1)}, u32[]{:S(2)}, u32[]{:S(2)}) collective-permute-start(bf16[192,2048]{1,0:T(8,128)(2,1)} %collective-permute-done.25.g_own), channel_id=1, source_target_pairs={{0,12},{1,13},{2,14},{3,15},{4,0},{5,1},{6,2},{7,3},{8,4},{9,5},{1... | collective-permute-start | bytes 2359304 | tf_op jit(solution)/shard_map/ppermute | solution.py:436
  162.8 46.4 %collective-permute-start.26 = (bf16[192,2048]{1,0:T(8,128)(2,1)}, bf16[192,2048]{1,0:T(8,128)(2,1)}, u32[]{:S(2)}, u32[]{:S(2)}) collective-permute-start(bf16[192,2048]{1,0:T(8,128)(2,1)} %collective-permute-done.25.g_own), channel_id=1, source_target_pairs={{0,2},{1,3},{2,0},{3,1},{4,6},{5,7},{6,4},{7,5},{8,10},{9,11},{10,... | collective-permute-start | bytes 2359304 | tf_op jit(solution)/shard_map/ppermute | solution.py:433
  172.7 36.6 %collective-permute-start.10 = (bf16[192,2048]{1,0:T(8,128)(2,1)}, bf16[192,2048]{1,0:T(8,128)(2,1)}, u32[]{:S(2)}, u32[]{:S(2)}) collective-permute-start(bf16[192,2048]{1,0:T(8,128)(2,1)} %collective-permute-done.8.g_y), channel_id=1, source_target_pairs={{0,1},{1,0},{2,3},{3,2},{4,5},{5,4},{6,7},{7,6},{8,9},{9,8},{10,11... | collective-permute-start | bytes 2359304 | tf_op jit(solution)/shard_map/ppermute | solution.py:430
  208.8 41.2 %collective-permute-start.27 = (bf16[192,2048]{1,0:T(8,128)(2,1)}, bf16[192,2048]{1,0:T(8,128)(2,1)S(1)}, u32[]{:S(2)}, u32[]{:S(2)}) collective-permute-start(bf16[192,2048]{1,0:T(8,128)(2,1)} %collective-permute-done.25.g_own), channel_id=1, source_target_pairs={{0,1},{1,0},{2,3},{3,2},{4,5},{5,4},{6,7},{7,6},{8,9},{9,8},{10,11... | collective-permute-start | bytes 2359304 | tf_op jit(solution)/shard_map/ppermute | solution.py:430
  209.3 41.2 %collective-permute-start.48 = (bf16[192,2048]{1,0:T(8,128)(2,1)}, bf16[192,2048]{1,0:T(8,128)(2,1)S(1)}, u32[]{:S(2)}, u32[]{:S(2)}) collective-permute-start(bf16[192,2048]{1,0:T(8,128)(2,1)} %collective-permute-done.29.n_own), channel_id=1, source_target_pairs={{0,12},{1,13},{2,14},{3,15},{4,0},{5,1},{6,2},{7,3},{8,4},{9,5},{1... | collective-permute-start | bytes 2359304 | tf_op jit(solution)/shard_map/ppermute | solution.py:436
  209.3 42.8 %collective-permute-start.31 = (bf16[192,2048]{1,0:T(8,128)(2,1)}, bf16[192,2048]{1,0:T(8,128)(2,1)S(1)}, u32[]{:S(2)}, u32[]{:S(2)}) collective-permute-start(bf16[192,2048]{1,0:T(8,128)(2,1)} %collective-permute-done.29.n_own), channel_id=1, source_target_pairs={{0,1},{1,0},{2,3},{3,2},{4,5},{5,4},{6,7},{7,6},{8,9},{9,8},{10,11... | collective-permute-start | bytes 2359304 | tf_op jit(solution)/shard_map/ppermute | solution.py:430
  209.4 42.7 %collective-permute-start.28 = (bf16[192,2048]{1,0:T(8,128)(2,1)}, bf16[192,2048]{1,0:T(8,128)(2,1)S(1)}, u32[]{:S(2)}, u32[]{:S(2)}) collective-permute-start(bf16[192,2048]{1,0:T(8,128)(2,1)} %collective-permute-done.26.g_y), channel_id=1, source_target_pairs={{0,1},{1,0},{2,3},{3,2},{4,5},{5,4},{6,7},{7,6},{8,9},{9,8},{10,11... | collective-permute-start | bytes 2359304 | tf_op jit(solution)/shard_map/ppermute | solution.py:430
  209.9 42.8 %collective-permute-start.32 = (bf16[192,2048]{1,0:T(8,128)(2,1)}, bf16[192,2048]{1,0:T(8,128)(2,1)S(1)}, u32[]{:S(2)}, u32[]{:S(2)}) collective-permute-start(bf16[192,2048]{1,0:T(8,128)(2,1)} %collective-permute-done.30.n_y), channel_id=1, source_target_pairs={{0,1},{1,0},{2,3},{3,2},{4,5},{5,4},{6,7},{7,6},{8,9},{9,8},{10,11... | collective-permute-start | bytes 2359304 | tf_op jit(solution)/shard_map/ppermute | solution.py:430
  250.0 34.5 %collective-permute-start.37 = (bf16[192,2048]{1,0:T(8,128)(2,1)S(1)}, bf16[192,2048]{1,0:T(8,128)(2,1)S(1)}, u32[]{:S(2)}, u32[]{:S(2)}) collective-permute-start(bf16[192,2048]{1,0:T(8,128)(2,1)S(1)} %copy-done.17), channel_id=1, source_target_pairs={{0,2},{1,3},{2,0},{3,1},{4,6},{5,7},{6,4},{7,5},{8,10},{9,11},{10,... | collective-permute-start | bytes 2359304 | tf_op jit(solution)/shard_map/ppermute | solution.py:433
  250.5 82.2 %collective-permute-start.41 = (bf16[192,2048]{1,0:T(8,128)(2,1)}, bf16[192,2048]{1,0:T(8,128)(2,1)S(1)}, u32[]{:S(2)}, u32[]{:S(2)}) collective-permute-start(bf16[192,2048]{1,0:T(8,128)(2,1)} %collective-permute-done.40.n_own), channel_id=1, source_target_pairs={{0,2},{1,3},{2,0},{3,1},{4,6},{5,7},{6,4},{7,5},{8,10},{9,11},{10,... | collective-permute-start | bytes 2359304 | tf_op jit(solution)/shard_map/ppermute | solution.py:433
  252.1 81.1 %collective-permute-start.46 = (bf16[192,2048]{1,0:T(8,128)(2,1)}, bf16[192,2048]{1,0:T(8,128)(2,1)S(1)}, u32[]{:S(2)}, u32[]{:S(2)}) collective-permute-start(bf16[192,2048]{1,0:T(8,128)(2,1)} %collective-permute-done.44.g_own), channel_id=1, source_target_pairs={{0,1},{1,0},{2,3},{3,2},{4,5},{5,4},{6,7},{7,6},{8,9},{9,8},{10,11... | collective-permute-start | bytes 2359304 | tf_op jit(solution)/shard_map/ppermute | solution.py:430
  252.1 52.1 %collective-permute-start.45 = (bf16[192,2048]{1,0:T(8,128)(2,1)}, bf16[192,2048]{1,0:T(8,128)(2,1)S(1)}, u32[]{:S(2)}, u32[]{:S(2)}) collective-permute-start(bf16[192,2048]{1,0:T(8,128)(2,1)} %collective-permute-done.44.g_own), channel_id=1, source_target_pairs={{0,2},{1,3},{2,0},{3,1},{4,6},{5,7},{6,4},{7,5},{8,10},{9,11},{10,... | collective-permute-start | bytes 2359304 | tf_op jit(solution)/shard_map/ppermute | solution.py:433
  253.5 67.0 %collective-permute-start.49 = (bf16[192,2048]{1,0:T(8,128)(2,1)S(1)}, bf16[192,2048]{1,0:T(8,128)(2,1)S(1)}, u32[]{:S(2)}, u32[]{:S(2)}) collective-permute-start(bf16[192,2048]{1,0:T(8,128)(2,1)S(1)} %collective-permute-done.48.n_own), channel_id=1, source_target_pairs={{0,2},{1,3},{2,0},{3,1},{4,6},{5,7},{6,4},{7,5},{8,10},{9,11},{10,... | collective-permute-start | bytes 2359304 | tf_op jit(solution)/shard_map/ppermute | solution.py:433
  284.5 48.8 %collective-permute-start.50 = (bf16[192,2048]{1,0:T(8,128)(2,1)S(1)}, bf16[192,2048]{1,0:T(8,128)(2,1)S(1)}, u32[]{:S(2)}, u32[]{:S(2)}) collective-permute-start(bf16[192,2048]{1,0:T(8,128)(2,1)S(1)} %collective-permute-done.48.n_own), channel_id=1, source_target_pairs={{0,1},{1,0},{2,3},{3,2},{4,5},{5,4},{6,7},{7,6},{8,9},{9,8},{10,11... | collective-permute-start | bytes 2359304 | tf_op jit(solution)/shard_map/ppermute | solution.py:430
  332.7 38.7 %collective-permute-start.38 = (bf16[192,2048]{1,0:T(8,128)(2,1)S(1)}, bf16[192,2048]{1,0:T(8,128)(2,1)S(1)}, u32[]{:S(2)}, u32[]{:S(2)}) collective-permute-start(bf16[192,2048]{1,0:T(8,128)(2,1)S(1)} %copy-done.17), channel_id=1, source_target_pairs={{0,1},{1,0},{2,3},{3,2},{4,5},{5,4},{6,7},{7,6},{8,9},{9,8},{10,11... | collective-permute-start | bytes 2359304 | tf_op jit(solution)/shard_map/ppermute | solution.py:430
  333.2 38.2 %collective-permute-start.42 = (bf16[192,2048]{1,0:T(8,128)(2,1)}, bf16[192,2048]{1,0:T(8,128)(2,1)S(1)}, u32[]{:S(2)}, u32[]{:S(2)}) collective-permute-start(bf16[192,2048]{1,0:T(8,128)(2,1)} %collective-permute-done.40.n_own), channel_id=1, source_target_pairs={{0,1},{1,0},{2,3},{3,2},{4,5},{5,4},{6,7},{7,6},{8,9},{9,8},{10,11... | collective-permute-start | bytes 2359304 | tf_op jit(solution)/shard_map/ppermute | solution.py:430
  333.2 38.2 %collective-permute-start.39 = (bf16[192,2048]{1,0:T(8,128)(2,1)S(1)}, bf16[192,2048]{1,0:T(8,128)(2,1)S(1)}, u32[]{:S(2)}, u32[]{:S(2)}) collective-permute-start(bf16[192,2048]{1,0:T(8,128)(2,1)S(1)} %collective-permute-done.37.g_y), channel_id=1, source_target_pairs={{0,1},{1,0},{2,3},{3,2},{4,5},{5,4},{6,7},{7,6},{8,9},{9,8},{10,11... | collective-permute-start | bytes 2359304 | tf_op jit(solution)/shard_map/ppermute | solution.py:430
  333.7 37.7 %collective-permute-start.43 = (bf16[192,2048]{1,0:T(8,128)(2,1)S(1)}, bf16[192,2048]{1,0:T(8,128)(2,1)S(1)}, u32[]{:S(2)}, u32[]{:S(2)}) collective-permute-start(bf16[192,2048]{1,0:T(8,128)(2,1)S(1)} %collective-permute-done.41.n_y), channel_id=1, source_target_pairs={{0,1},{1,0},{2,3},{3,2},{4,5},{5,4},{6,7},{7,6},{8,9},{9,8},{10,11... | collective-permute-start | bytes 2359304 | tf_op jit(solution)/shard_map/ppermute | solution.py:430
  334.6 99.8 %collective-permute-start.23 = (bf16[2,384,2048]{2,1,0:T(8,128)(2,1)}, bf16[2,384,2048]{2,1,0:T(8,128)(2,1)}, u32[]{:S(2)}, u32[]{:S(2)}) collective-permute-start(bf16[2,384,2048]{2,1,0:T(8,128)(2,1)} %get-tuple-element.101), channel_id=1, source_target_pairs={{0,1},{1,0},{2,3},{3,2},{4,5},{5,4},{6,7},{7,6},{8,9},{9,8},{10,11... | collective-permute-start | bytes 9437192 | tf_op jit(solution)/shard_map/ppermute | solution.py:430
  371.4 66.0 %collective-permute-start.33 = (bf16[2,384,2048]{2,1,0:T(8,128)(2,1)}, bf16[2,384,2048]{2,1,0:T(8,128)(2,1)}, u32[]{:S(2)}, u32[]{:S(2)}) collective-permute-start(bf16[2,384,2048]{2,1,0:T(8,128)(2,1)} %get-tuple-element.113), channel_id=1, source_target_pairs={{0,1},{1,0},{2,3},{3,2},{4,5},{5,4},{6,7},{7,6},{8,9},{9,8},{10,11... | collective-permute-start | bytes 9437192 | tf_op jit(solution)/shard_map/ppermute | solution.py:430
  411.9 60.1 %collective-permute-start.78 = (bf16[640,2048]{1,0:T(8,128)(2,1)}, bf16[640,2048]{1,0:T(8,128)(2,1)}, u32[]{:S(2)}, u32[]{:S(2)}) collective-permute-start(bf16[640,2048]{1,0:T(8,128)(2,1)} %add_convert_fusion), channel_id=1, source_target_pairs={{0,16},{16,0},{1,17},{17,1},{2,18},{18,2},{3,19},{19,3},{4,20},{20... | collective-permute-start | bytes 7864328 | tf_op jit(solution)/shard_map/ppermute | solution.py:446
  414.7 60.9 %collective-permute-start.54 = (bf16[2,384,2048]{2,1,0:T(8,128)(2,1)}, bf16[2,384,2048]{2,1,0:T(8,128)(2,1)}, u32[]{:S(2)}, u32[]{:S(2)}) collective-permute-start(bf16[2,384,2048]{2,1,0:T(8,128)(2,1)} %get-tuple-element.137), channel_id=1, source_target_pairs={{0,1},{1,0},{2,3},{3,2},{4,5},{5,4},{6,7},{7,6},{8,9},{9,8},{10,11... | collective-permute-start | bytes 9437192 | tf_op jit(solution)/shard_map/ppermute | solution.py:430
  426.4 123.8 %collective-permute-start.58 = (f32[16,64,896]{2,1,0:T(8,128)}, f32[16,64,896]{2,1,0:T(8,128)}, u32[]{:S(2)}, u32[]{:S(2)}) collective-permute-start(f32[16,64,896]{2,1,0:T(8,128)} %get-tuple-element.143), channel_id=1, source_target_pairs={{0,16},{16,0},{1,17},{17,1},{2,18},{18,2},{3,19},{19,3},{4,20},{20... | collective-permute-start | bytes 11010056 | tf_op jit(solution)/shard_map/ppermute | solution.py:446
  434.5 134.7 %collective-permute-start.52 = (bf16[2,384,2048]{2,1,0:T(8,128)(2,1)}, bf16[2,384,2048]{2,1,0:T(8,128)(2,1)}, u32[]{:S(2)}, u32[]{:S(2)}) collective-permute-start(bf16[2,384,2048]{2,1,0:T(8,128)(2,1)} %get-tuple-element.135), channel_id=1, source_target_pairs={{0,1},{1,0},{2,3},{3,2},{4,5},{5,4},{6,7},{7,6},{8,9},{9,8},{10,11... | collective-permute-start | bytes 9437192 | tf_op jit(solution)/shard_map/ppermute | solution.py:430
  441.6 209.6 %collective-permute-start.34 = (bf16[2,192,2048]{2,1,0:T(8,128)(2,1)}, bf16[2,192,2048]{2,1,0:T(8,128)(2,1)}, u32[]{:S(2)}, u32[]{:S(2)}) collective-permute-start(bf16[2,192,2048]{2,1,0:T(8,128)(2,1)} %add_convert_fusion.6), channel_id=1, source_target_pairs={{0,2},{1,3},{2,0},{3,1},{4,6},{5,7},{6,4},{7,5},{8,10},{9,11},{10,... | collective-permute-start | bytes 4718600 | tf_op jit(solution)/shard_map/ppermute | solution.py:433
  478.9 96.7 %collective-permute-start.55 = (bf16[2,192,2048]{2,1,0:T(8,128)(2,1)}, bf16[2,192,2048]{2,1,0:T(8,128)(2,1)}, u32[]{:S(2)}, u32[]{:S(2)}) collective-permute-start(bf16[2,192,2048]{2,1,0:T(8,128)(2,1)} %add_convert_fusion.3), channel_id=1, source_target_pairs={{0,2},{1,3},{2,0},{3,1},{4,6},{5,7},{6,4},{7,5},{8,10},{9,11},{10,... | collective-permute-start | bytes 4718600 | tf_op jit(solution)/shard_map/ppermute | solution.py:433
  575.6 80.3 %collective-permute-start.53 = (bf16[2,192,2048]{2,1,0:T(8,128)(2,1)S(1)}, bf16[2,192,2048]{2,1,0:T(8,128)(2,1)S(1)}, u32[]{:S(2)}, u32[]{:S(2)}) collective-permute-start(bf16[2,192,2048]{2,1,0:T(8,128)(2,1)S(1)} %add_convert_fusion.4), channel_id=1, source_target_pairs={{0,2},{1,3},{2,0},{3,1},{4,6},{5,7},{6,4},{7,5},{8,10},{9,11},{10,... | collective-permute-start | bytes 4718600 | tf_op jit(solution)/shard_map/ppermute | solution.py:433
  579.9 76.1 %collective-permute-start.56 = (bf16[2,192,2048]{2,1,0:T(8,128)(2,1)S(1)}, bf16[2,192,2048]{2,1,0:T(8,128)(2,1)S(1)}, u32[]{:S(2)}, u32[]{:S(2)}) collective-permute-start(bf16[2,192,2048]{2,1,0:T(8,128)(2,1)S(1)} %add_convert_fusion.2), channel_id=1, source_target_pairs={{0,12},{1,13},{2,14},{3,15},{4,0},{5,1},{6,2},{7,3},{8,4},{9,5},{1... | collective-permute-start | bytes 4718600 | tf_op jit(solution)/shard_map/ppermute | solution.py:436
  587.6 71.2 %collective-permute-start.24 = (bf16[2,192,2048]{2,1,0:T(8,128)(2,1)S(1)}, bf16[2,192,2048]{2,1,0:T(8,128)(2,1)S(1)}, u32[]{:S(2)}, u32[]{:S(2)}) collective-permute-start(bf16[2,192,2048]{2,1,0:T(8,128)(2,1)S(1)} %add_convert_fusion.7), channel_id=1, source_target_pairs={{0,2},{1,3},{2,0},{3,1},{4,6},{5,7},{6,4},{7,5},{8,10},{9,11},{10,... | collective-permute-start | bytes 4718600 | tf_op jit(solution)/shard_map/ppermute | solution.py:433
  596.1 53.0 %collective-permute-start.75 = (bf16[2,64,896]{2,1,0:T(8,128)(2,1)S(1)}, bf16[2,64,896]{2,1,0:T(8,128)(2,1)S(1)}, u32[]{:S(2)}, u32[]{:S(2)}) collective-permute-start(bf16[2,64,896]{2,1,0:T(8,128)(2,1)S(1)} %get-tuple-element.225), channel_id=1, source_target_pairs={{0,2},{1,3},{2,0},{3,1},{4,6},{5,7},{6,4},{7,5},{8,10},{9,11},{10,... | collective-permute-start | bytes 688136 | tf_op jit(solution)/shard_map/ppermute | solution.py:433
  651.2 50.4 %collective-permute-start.65 = (bf16[4,64,896]{2,1,0:T(8,128)(2,1)S(1)}, bf16[4,64,896]{2,1,0:T(8,128)(2,1)S(1)}, u32[]{:S(2)}, u32[]{:S(2)}) collective-permute-start(bf16[4,64,896]{2,1,0:T(8,128)(2,1)S(1)} %add_convert_fusion.10), channel_id=1, source_target_pairs={{0,12},{1,13},{2,14},{3,15},{4,0},{5,1},{6,2},{7,3},{8,4},{9,5},{1... | collective-permute-start | bytes 1376264 | tf_op jit(solution)/shard_map/ppermute | solution.py:436
  656.0 113.8 %collective-permute-start.35 = (bf16[2,192,2048]{2,1,0:T(8,128)(2,1)S(1)}, bf16[2,192,2048]{2,1,0:T(8,128)(2,1)S(1)}, u32[]{:S(2)}, u32[]{:S(2)}) collective-permute-start(bf16[2,192,2048]{2,1,0:T(8,128)(2,1)S(1)} %add_convert_fusion.5), channel_id=1, source_target_pairs={{0,4},{1,5},{2,6},{3,7},{4,8},{5,9},{6,10},{7,11},{8,12},{9,13},{1... | collective-permute-start | bytes 4718600 | tf_op jit(solution)/shard_map/ppermute | solution.py:436
  658.8 111.6 %collective-permute-start.57 = (bf16[2,192,2048]{2,1,0:T(8,128)(2,1)S(1)}, bf16[2,192,2048]{2,1,0:T(8,128)(2,1)S(1)}, u32[]{:S(2)}, u32[]{:S(2)}) collective-permute-start(bf16[2,192,2048]{2,1,0:T(8,128)(2,1)S(1)} %add_convert_fusion.1), channel_id=1, source_target_pairs={{0,12},{1,13},{2,14},{3,15},{4,0},{5,1},{6,2},{7,3},{8,4},{9,5},{1... | collective-permute-start | bytes 4718600 | tf_op jit(solution)/shard_map/ppermute | solution.py:436
  664.9 92.7 %collective-permute-start.60 = (bf16[4,64,896]{2,1,0:T(8,128)(2,1)S(1)}, bf16[4,64,896]{2,1,0:T(8,128)(2,1)S(1)}, u32[]{:S(2)}, u32[]{:S(2)}) collective-permute-start(bf16[4,64,896]{2,1,0:T(8,128)(2,1)S(1)} %add_convert_fusion.11), channel_id=1, source_target_pairs={{0,8},{1,9},{2,10},{3,11},{4,12},{5,13},{6,14},{7,15},{8,0},{9,1},... | collective-permute-start | bytes 1376264 | tf_op jit(solution)/shard_map/ppermute | solution.py:436
  665.1 140.0 %collective-permute-start.77 = (bf16[4,64,896]{2,1,0:T(8,128)(2,1)S(1)}, bf16[4,64,896]{2,1,0:T(8,128)(2,1)S(1)}, u32[]{:S(2)}, u32[]{:S(2)}) collective-permute-start(bf16[4,64,896]{2,1,0:T(8,128)(2,1)S(1)} %bitcast.165), channel_id=1, source_target_pairs={{0,16},{16,0},{1,17},{17,1},{2,18},{18,2},{3,19},{19,3},{4,20},{20... | collective-permute-start | bytes 1376264 | tf_op jit(solution)/shard_map/ppermute | solution.py:446
  701.6 56.5 %collective-permute-start.71 = (bf16[2,64,896]{2,1,0:T(8,128)(2,1)S(1)}, bf16[2,64,896]{2,1,0:T(8,128)(2,1)S(1)}, u32[]{:S(2)}, u32[]{:S(2)}) collective-permute-start(bf16[2,64,896]{2,1,0:T(8,128)(2,1)S(1)} %get-tuple-element.221), channel_id=1, source_target_pairs={{0,2},{1,3},{2,0},{3,1},{4,6},{5,7},{6,4},{7,5},{8,10},{9,11},{10,... | collective-permute-start | bytes 688136 | tf_op jit(solution)/shard_map/ppermute | solution.py:433
  (100 other events, 1443.0 us)
